TPU v7x, 512 devices: a whole 4x4x16 slice. The times are simulated.
512 devices in a mesh: layer: 64 (over x, z), row: 8 (over y, core).
Axes of the slice: x: 4, y: 4, z: 16, core: 2. Of those that a mesh axis runs over, the one named last changes fastest.
Arguments:
- coupling: bfloat16 [64, 1024, 1024], P('layer', 'row'), may hold values from -1 to 1, as said below
- band_off: int32 [64], P('layer'), may hold values from 0 to 32
- band_width: int32 [64], P('layer'), may hold values from 1 to 3
- incident: float32 [32, 1024], P(None, 'row'), may hold values from -6 to 6
- cotangent: float32 [32, 1024], P(None, 'row'), may hold values from -6 to 6
Outputs:
- transmitted: float32 [64, 32, 1024], P('layer', None, 'row')
- adjoint: float32 [64, 32, 1024], P('layer', None, 'row')
Inputs may be any that keep to these rules, and one draw needn't show every extreme that they name: coupling is antisymmetric in its last two dimensions.
All inputs are finite; a program needn't handle non-finite values.
Results may differ from a plain program's by a relative error of at most 0.012.
The roundings to bfloat16 on the way count: a program that leaves them out, or rounds other values in their place, can miss the bound.
Values may be sent and summed in bfloat16 or wider, within the bound.
A program may use at most 64 MiB of HBM per device.

v0:
```python
import jax
import jax.numpy as jnp
from jax import lax
from jax.sharding import PartitionSpec as P

BLOCK = 16
GROUP = 8


def partner(array, axis, bit):
    return lax.ppermute(array, axis, [(i, i ^ 1 << bit) for i in range(lax.axis_size(axis))])


def from_behind(block, axis, distance):
    devices = range(lax.axis_size(axis))
    route = [(i - distance, i) for i in devices if i - distance in devices]
    return lax.ppermute(block, axis, route)


def band_mask(row_ids, col_ids, offset, half_width):
    diff = col_ids[None, :] // BLOCK - row_ids[:, None] // BLOCK
    return (jnp.abs(diff - offset) <= half_width) | (jnp.abs(diff + offset) <= half_width)


def on_device(coupling, band_off, band_width, incident, cotangent):
    panel_rows = coupling.shape[1]
    orders = coupling.shape[2]
    row_index = lax.axis_index("row")
    layer_index = lax.axis_index("layer")
    row_ids = row_index * panel_rows + jnp.arange(panel_rows, dtype=jnp.int32)
    col_ids = jnp.arange(orders, dtype=jnp.int32)
    local_coupling = coupling[0]
    banded = jnp.where(
        band_mask(row_ids, col_ids, band_off[0], band_width[0]),
        local_coupling,
        jnp.zeros_like(local_coupling),
    )
    identity = (col_ids[None, :] == row_ids[:, None]).astype(jnp.float32)
    whole_band = lax.all_gather(banded, "row", axis=0, tiled=True)
    whole_identity = (col_ids[None, :] == col_ids[:, None]).astype(jnp.float32)
    section = (whole_identity + whole_band.astype(jnp.float32) / 4.0).astype(jnp.bfloat16)
    for divisor in (3.0, 2.0):
        section = (
            whole_identity
            + jnp.dot(whole_band, section, preferred_element_type=jnp.float32) / divisor
        ).astype(jnp.bfloat16)
    section = (identity + jnp.dot(banded, section, preferred_element_type=jnp.float32)).astype(
        jnp.bfloat16
    )
    upper_side = layer_index & 1 == 1
    received = partner(section, "layer", 0)
    later_map = jnp.where(upper_side, section, received)
    earlier_map = jnp.where(upper_side, received, section)
    empty_map = jnp.zeros((panel_rows, orders), jnp.float32)
    composed = jnp.dot(
        later_map,
        lax.all_gather(earlier_map, "row", axis=0, tiled=True),
        preferred_element_type=jnp.float32,
    )
    for level in range(1, GROUP.bit_length() - 1):
        upper_side = layer_index >> level & 1 == 1
        received = partner(composed, "layer", level)
        later_level = jnp.where(upper_side, composed, received)
        earlier_level = jnp.where(upper_side, received, composed)

        def add_level(carry_sum, block_rows, first_row, later_level=later_level):
            return jnp.dot(
                later_level,
                block_rows,
                precision=lax.Precision.HIGHEST,
                preferred_element_type=jnp.float32,
            )

        composed = add_level(
            empty_map, lax.all_gather(earlier_level, "row", axis=0, tiled=True), jnp.int32(0)
        )
    groups = lax.axis_size("layer") // GROUP
    group_index = layer_index // GROUP
    field_count = incident.shape[0]
    empty_field = jnp.zeros((field_count, panel_rows), jnp.float32)
    forward_field = incident
    adjoint_field = cotangent
    forward_kept = empty_field
    adjoint_kept = empty_field
    for step_num in range(groups):
        forward_done = lax.dot_general(
            lax.all_gather(forward_field, "row", axis=1, tiled=True),
            composed,
            (((1,), (1,)), ((), ())),
            precision=lax.Precision.HIGHEST,
            preferred_element_type=jnp.float32,
        )
        forward_kept = jnp.where(group_index == step_num, forward_done, forward_kept)
        if step_num + 1 < groups:
            forward_field = from_behind(forward_done, "layer", GROUP)
    for step_num in range(groups):
        partial_term = jnp.dot(
            adjoint_field,
            composed,
            precision=lax.Precision.HIGHEST,
            preferred_element_type=jnp.float32,
        )
        adjoint_done = lax.psum_scatter(partial_term, "row", scatter_dimension=1, tiled=True)
        adjoint_kept = jnp.where(group_index == groups - 1 - step_num, adjoint_done, adjoint_kept)
        if step_num + 1 < groups:
            adjoint_field = from_behind(adjoint_done, "layer", -GROUP)
    return (forward_kept[None], adjoint_kept[None])


def solution(mesh):
    in_specs = (P("layer", "row", None), P("layer"), P("layer"), P(None, "row"), P(None, "row"))
    out_specs = (P("layer", None, "row"), P("layer", None, "row"))
    return jax.shard_map(
        on_device, mesh=mesh, in_specs=in_specs, out_specs=out_specs, check_vma=False
    )
```

profile of v0, /device:TPU:1, one launch (start us, length us, event | category | flops | bytes accessed | tf_op | source)
XLA Modules:
  0.0 707.2 jit_solution(14201648366117297181)
XLA Ops:
  8.6 1.9 fusion.23
  10.6 38.8 %all-gather.5.cloned.1.call-done = bf16[1024,1024]{1,0:T(8,128)(2,1)} async-done(((bf16[128,1024]{1,0:T(8,128)(2,1)}), bf16[1024,1024]{1,0:T(8,128)(2,1)}) %all-gather.5.cloned.1.call-update) | async-done | bytes 2097168 | tf_op jit(solution)/shard_map/all_gather | solution.py:39
  49.4 7.4 %fusion.2 = bf16[1024,1024]{1,0:T(8,128)(2,1)S(1)} fusion(bf16[1024,1024]{1,0:T(8,128)(2,1)} %all-gather.5.cloned.1.call-done), kind=kOutput, calls=%fused_computation.5 | convolution fusion | flops 4311744512 | bytes 4194304 | tf_op jit(solution)/shard_map/dot_general | solution.py:45
  57.3 3.2 collective-permute-start
  60.5 6.3 collective-permute-done
  67.5 34.4 %all-gather.7.cloned.1.call-done = bf16[1024,1024]{1,0:T(8,128)(2,1)} async-done(((bf16[128,1024]{1,0:T(8,128)(2,1)}), bf16[1024,1024]{1,0:T(8,128)(2,1)}) %all-gather.7.cloned.1.call-update) | async-done | bytes 2097168 | tf_op jit(solution)/shard_map/all_gather | solution.py:57
  101.9 2.0 fusion.24
  104.0 4.2 collective-permute-start.1
  108.2 23.0 %collective-permute-done.1 = f32[128,1024]{1,0:T(8,128)S(1)} collective-permute-done((f32[128,1024]{1,0:T(8,128)S(1)}, f32[128,1024]{1,0:T(8,128)S(1)}, u32[]{:S(2)}, u32[]{:S(2)}) %collective-permute-start.1) | collective-permute-done | bytes 524320 | tf_op jit(solution)/shard_map/ppermute | solution.py:11
  132.1 41.2 %all-gather.9.cloned.1.call-done = f32[1024,1024]{1,0:T(8,128)} async-done(((f32[128,1024]{1,0:T(8,128)}), f32[1024,1024]{1,0:T(8,128)}) %all-gather.9.cloned.1.call-update) | async-done | bytes 4194320 | tf_op jit(solution)/shard_map/all_gather | solution.py:75
  173.3 4.6 fusion.20
  177.9 7.4 %collective-permute-start.2 = (f32[128,1024]{1,0:T(8,128)S(1)}, f32[128,1024]{1,0:T(8,128)S(1)}, u32[]{:S(2)}, u32[]{:S(2)}) collective-permute-start(f32[128,1024]{1,0:T(8,128)S(1)} %fusion.20), channel_id=1, source_target_pairs={{0,32},{8,40},{16,48},{24,56},{32,0},{40,8},{48,16},{56,24},{64,96... | collective-permute-start | bytes 1572872 | tf_op jit(solution)/shard_map/ppermute | solution.py:11
  185.3 45.5 %collective-permute-done.2 = f32[128,1024]{1,0:T(8,128)S(1)} collective-permute-done((f32[128,1024]{1,0:T(8,128)S(1)}, f32[128,1024]{1,0:T(8,128)S(1)}, u32[]{:S(2)}, u32[]{:S(2)}) %collective-permute-start.2) | collective-permute-done | bytes 524320 | tf_op jit(solution)/shard_map/ppermute | solution.py:11
  231.8 40.5 %all-gather.11.cloned.1.call-done = f32[1024,1024]{1,0:T(8,128)} async-done(((f32[128,1024]{1,0:T(8,128)}), f32[1024,1024]{1,0:T(8,128)}) %all-gather.11.cloned.1.call-update) | async-done | bytes 4194320 | tf_op jit(solution)/shard_map/all_gather | solution.py:75
  272.3 4.6 fusion.18
  278.0 36.7 %reduce-scatter.9.cloned.1.call-done = f32[32,128]{1,0:T(8,128)} async-done(((f32[32,1024]{1,0:T(8,128)}), f32[32,128]{1,0:T(8,128)}) %reduce-scatter.9.cloned.1.call-update) | async-done | bytes 16400 | tf_op jit(solution)/shard_map/reduce_scatter | solution.py:103
  314.7 1.3 collective-permute-start.10
  316.0 12.1 %collective-permute-done.10 = f32[32,128]{1,0:T(8,128)S(1)} collective-permute-done((f32[32,128]{1,0:T(8,128)}, f32[32,128]{1,0:T(8,128)S(1)}, u32[]{:S(2)}, u32[]{:S(2)}) %collective-permute-start.10) | collective-permute-done | bytes 16416 | tf_op jit(solution)/shard_map/ppermute | solution.py:17
  329.2 39.5 %reduce-scatter.11.cloned.1.call-done = f32[32,128]{1,0:T(8,128)} async-done(((f32[32,1024]{1,0:T(8,128)}), f32[32,128]{1,0:T(8,128)}) %reduce-scatter.11.cloned.1.call-update) | async-done | bytes 16400 | tf_op jit(solution)/shard_map/reduce_scatter | solution.py:103
  368.7 1.3 collective-permute-start.11
  370.0 12.1 %collective-permute-done.11 = f32[32,128]{1,0:T(8,128)S(1)} collective-permute-done((f32[32,128]{1,0:T(8,128)}, f32[32,128]{1,0:T(8,128)S(1)}, u32[]{:S(2)}, u32[]{:S(2)}) %collective-permute-start.11) | collective-permute-done | bytes 16416 | tf_op jit(solution)/shard_map/ppermute | solution.py:17
  383.2 39.5 %reduce-scatter.13.cloned.1.call-done = f32[32,128]{1,0:T(8,128)} async-done(((f32[32,1024]{1,0:T(8,128)}), f32[32,128]{1,0:T(8,128)}) %reduce-scatter.13.cloned.1.call-update) | async-done | bytes 16400 | tf_op jit(solution)/shard_map/reduce_scatter | solution.py:103
  422.7 1.3 collective-permute-start.12
  424.0 14.9 %all_gather.40 = f32[32,1024]{1,0:T(8,128)S(1)} all-gather(f32[32,128]{1,0:T(8,128)S(1)} %copy-done.2), channel_id=1, replica_groups=mesh['layer'=64,'row'=8] {'row'}, dimensions={1}, use_global_device_ids=true | all-gather | bytes 147456 | tf_op jit(solution)/shard_map/all_gather | solution.py:87
  440.6 13.1 %collective-permute-start.3 = (f32[32,128]{1,0:T(8,128)S(1)}, f32[32,128]{1,0:T(8,128)S(1)}, u32[]{:S(2)}, u32[]{:S(2)}) collective-permute-start(f32[32,128]{1,0:T(8,128)S(1)} %convolution_bitcast_fusion.1), channel_id=1, source_target_pairs={{0,64},{8,72},{16,80},{24,88},{32,96},{40,104},{48,112},{56,120},{... | collective-permute-start | bytes 49160 | tf_op jit(solution)/shard_map/ppermute | solution.py:17
  454.7 14.3 %all_gather.41 = f32[32,1024]{1,0:T(8,128)S(1)} all-gather(f32[32,128]{1,0:T(8,128)S(1)} %collective-permute-done.3), channel_id=1, replica_groups=mesh['layer'=64,'row'=8] {'row'}, dimensions={1}, use_global_device_ids=true | all-gather | bytes 147456 | tf_op jit(solution)/shard_map/all_gather | solution.py:87
  469.0 9.2 %reduce-scatter.15.cloned.1.call-done = f32[32,128]{1,0:T(8,128)} async-done(((f32[32,1024]{1,0:T(8,128)}), f32[32,128]{1,0:T(8,128)}) %reduce-scatter.15.cloned.1.call-update) | async-done | bytes 16400 | tf_op jit(solution)/shard_map/reduce_scatter | solution.py:103
  478.2 1.3 collective-permute-start.13
  480.2 12.8 %collective-permute-start.4 = (f32[32,128]{1,0:T(8,128)S(1)}, f32[32,128]{1,0:T(8,128)S(1)}, u32[]{:S(2)}, u32[]{:S(2)}) collective-permute-start(f32[32,128]{1,0:T(8,128)S(1)} %fusion.35), channel_id=1, source_target_pairs={{0,64},{8,72},{16,80},{24,88},{32,96},{40,104},{48,112},{56,120},{... | collective-permute-start | bytes 49160 | tf_op jit(solution)/shard_map/ppermute | solution.py:17
  494.2 15.9 %all_gather.42 = f32[32,1024]{1,0:T(8,128)S(1)} all-gather(f32[32,128]{1,0:T(8,128)S(1)} %collective-permute-done.4), channel_id=1, replica_groups=mesh['layer'=64,'row'=8] {'row'}, dimensions={1}, use_global_device_ids=true | all-gather | bytes 147456 | tf_op jit(solution)/shard_map/all_gather | solution.py:87
  510.7 13.2 %collective-permute-start.5 = (f32[32,128]{1,0:T(8,128)S(1)}, f32[32,128]{1,0:T(8,128)S(1)}, u32[]{:S(2)}, u32[]{:S(2)}) collective-permute-start(f32[32,128]{1,0:T(8,128)S(1)} %fusion.36), channel_id=1, source_target_pairs={{0,64},{8,72},{16,80},{24,88},{32,96},{40,104},{48,112},{56,120},{... | collective-permute-start | bytes 49160 | tf_op jit(solution)/shard_map/ppermute | solution.py:17
  523.9 9.2 %reduce-scatter.17.cloned.1.call-done = f32[32,128]{1,0:T(8,128)} async-done(((f32[32,1024]{1,0:T(8,128)}), f32[32,128]{1,0:T(8,128)}) %reduce-scatter.17.cloned.1.call-update) | async-done | bytes 16400 | tf_op jit(solution)/shard_map/reduce_scatter | solution.py:103
  533.2 1.4 collective-permute-start.14
  534.6 14.7 %all_gather.43 = f32[32,1024]{1,0:T(8,128)S(1)} all-gather(f32[32,128]{1,0:T(8,128)S(1)} %collective-permute-done.5), channel_id=1, replica_groups=mesh['layer'=64,'row'=8] {'row'}, dimensions={1}, use_global_device_ids=true | all-gather | bytes 147456 | tf_op jit(solution)/shard_map/all_gather | solution.py:87
  551.0 13.2 %collective-permute-start.6 = (f32[32,128]{1,0:T(8,128)S(1)}, f32[32,128]{1,0:T(8,128)S(1)}, u32[]{:S(2)}, u32[]{:S(2)}) collective-permute-start(f32[32,128]{1,0:T(8,128)S(1)} %fusion.37), channel_id=1, source_target_pairs={{0,64},{8,72},{16,80},{24,88},{32,96},{40,104},{48,112},{56,120},{... | collective-permute-start | bytes 49160 | tf_op jit(solution)/shard_map/ppermute | solution.py:17
  565.1 14.6 %all_gather.44 = f32[32,1024]{1,0:T(8,128)S(1)} all-gather(f32[32,128]{1,0:T(8,128)S(1)} %collective-permute-done.6), channel_id=1, replica_groups=mesh['layer'=64,'row'=8] {'row'}, dimensions={1}, use_global_device_ids=true | all-gather | bytes 147456 | tf_op jit(solution)/shard_map/all_gather | solution.py:87
  579.7 9.1 %reduce-scatter.19.cloned.1.call-done = f32[32,128]{1,0:T(8,128)} async-done(((f32[32,1024]{1,0:T(8,128)}), f32[32,128]{1,0:T(8,128)}) %reduce-scatter.19.cloned.1.call-update) | async-done | bytes 16400 | tf_op jit(solution)/shard_map/reduce_scatter | solution.py:103
  588.7 1.4 collective-permute-start.15
  590.8 12.7 %collective-permute-start.7 = (f32[32,128]{1,0:T(8,128)S(1)}, f32[32,128]{1,0:T(8,128)S(1)}, u32[]{:S(2)}, u32[]{:S(2)}) collective-permute-start(f32[32,128]{1,0:T(8,128)S(1)} %fusion.38), channel_id=1, source_target_pairs={{0,64},{8,72},{16,80},{24,88},{32,96},{40,104},{48,112},{56,120},{... | collective-permute-start | bytes 49160 | tf_op jit(solution)/shard_map/ppermute | solution.py:17
  604.6 15.9 %all_gather.45 = f32[32,1024]{1,0:T(8,128)S(1)} all-gather(f32[32,128]{1,0:T(8,128)S(1)} %collective-permute-done.7), channel_id=1, replica_groups=mesh['layer'=64,'row'=8] {'row'}, dimensions={1}, use_global_device_ids=true | all-gather | bytes 147456 | tf_op jit(solution)/shard_map/all_gather | solution.py:87
  621.2 13.3 %collective-permute-start.8 = (f32[32,128]{1,0:T(8,128)S(1)}, f32[32,128]{1,0:T(8,128)S(1)}, u32[]{:S(2)}, u32[]{:S(2)}) collective-permute-start(f32[32,128]{1,0:T(8,128)S(1)} %fusion.39), channel_id=1, source_target_pairs={{0,64},{8,72},{16,80},{24,88},{32,96},{40,104},{48,112},{56,120},{... | collective-permute-start | bytes 49160 | tf_op jit(solution)/shard_map/ppermute | solution.py:17
  634.4 9.1 %reduce-scatter.21.cloned.1.call-done = f32[32,128]{1,0:T(8,128)} async-done(((f32[32,1024]{1,0:T(8,128)}), f32[32,128]{1,0:T(8,128)}) %reduce-scatter.21.cloned.1.call-update) | async-done | bytes 16400 | tf_op jit(solution)/shard_map/reduce_scatter | solution.py:103
  643.5 1.3 collective-permute-start.16
  644.8 14.7 %all_gather.46 = f32[32,1024]{1,0:T(8,128)S(1)} all-gather(f32[32,128]{1,0:T(8,128)S(1)} %collective-permute-done.8), channel_id=1, replica_groups=mesh['layer'=64,'row'=8] {'row'}, dimensions={1}, use_global_device_ids=true | all-gather | bytes 147456 | tf_op jit(solution)/shard_map/all_gather | solution.py:87
  661.2 13.2 %collective-permute-start.9 = (f32[32,128]{1,0:T(8,128)S(1)}, f32[32,128]{1,0:T(8,128)S(1)}, u32[]{:S(2)}, u32[]{:S(2)}) collective-permute-start(f32[32,128]{1,0:T(8,128)S(1)} %fusion.40), channel_id=1, source_target_pairs={{0,64},{8,72},{16,80},{24,88},{32,96},{40,104},{48,112},{56,120},{... | collective-permute-start | bytes 49160 | tf_op jit(solution)/shard_map/ppermute | solution.py:17
  675.3 14.6 %all_gather.47 = f32[32,1024]{1,0:T(8,128)S(1)} all-gather(f32[32,128]{1,0:T(8,128)S(1)} %collective-permute-done.9), channel_id=1, replica_groups=mesh['layer'=64,'row'=8] {'row'}, dimensions={1}, use_global_device_ids=true | all-gather | bytes 147456 | tf_op jit(solution)/shard_map/all_gather | solution.py:87
  691.2 7.8 %reduce-scatter.23.cloned.1.call-done = f32[32,128]{1,0:T(8,128)} async-done(((f32[32,1024]{1,0:T(8,128)}), f32[32,128]{1,0:T(8,128)}) %reduce-scatter.23.cloned.1.call-update) | async-done | bytes 16400 | tf_op jit(solution)/shard_map/reduce_scatter | solution.py:103
  699.0 1.3 select_bitcast_fusion
  (77 shorter events, 20.1 us)
Async XLA Ops:
  7.2 269.7 %copy-start = (f32[32,128]{1,0:T(8,128)S(1)}, f32[32,128]{1,0:T(8,128)}, u32[]{:S(2)}) copy-start(f32[32,128]{1,0:T(8,128)} %param.9) | copy-start | bytes 49156
  7.2 42.2 %all-gather.5.cloned.1.call-start = ((), (), s32[]{:S(2)}) async-start(), calls=%async_computation.8 | async-start | bytes 2359296 | tf_op jit(solution)/shard_map/all_gather | solution.py:39
  10.5 91.4 %all-gather.7.cloned.1.call-start = ((), (), s32[]{:S(2)}) async-start(), calls=%async_computation.9 | async-start | bytes 2359296 | tf_op jit(solution)/shard_map/all_gather | solution.py:57
  10.6 46.2 %copy-start.1 = (bf16[128,1024]{1,0:T(8,128)(2,1)S(1)}, bf16[128,1024]{1,0:T(8,128)(2,1)}, u32[]{:S(2)}) copy-start(bf16[128,1024]{1,0:T(8,128)(2,1)} %fusion.23) | copy-start | bytes 786436
  57.3 9.5 %collective-permute-start = (bf16[128,1024]{1,0:T(8,128)(2,1)S(1)}, bf16[128,1024]{1,0:T(8,128)(2,1)S(1)}, u32[]{:S(2)}, u32[]{:S(2)}) collective-permute-start(bf16[128,1024]{1,0:T(8,128)(2,1)S(1)} %fusion.12), channel_id=1, source_target_pairs={{0,8},{8,0},{16,24},{24,16},{32,40},{40,32},{48,56},{56,48},{64,72... | collective-permute-start | bytes 786440 | tf_op jit(solution)/shard_map/ppermute | solution.py:11
  67.5 105.8 %all-gather.9.cloned.1.call-start = ((), (), s32[]{:S(2)}) async-start(), calls=%async_computation.10 | async-start | bytes 4718592 | tf_op jit(solution)/shard_map/all_gather | solution.py:75
  104.0 27.2 %collective-permute-start.1 = (f32[128,1024]{1,0:T(8,128)S(1)}, f32[128,1024]{1,0:T(8,128)S(1)}, u32[]{:S(2)}, u32[]{:S(2)}) collective-permute-start(f32[128,1024]{1,0:T(8,128)S(1)} %fusion.24), channel_id=1, source_target_pairs={{0,16},{8,24},{16,0},{24,8},{32,48},{40,56},{48,32},{56,40},{64,80... | collective-permute-start | bytes 1572872 | tf_op jit(solution)/shard_map/ppermute | solution.py:11
  132.1 140.2 %all-gather.11.cloned.1.call-start = ((), (), s32[]{:S(2)}) async-start(), calls=%async_computation.11 | async-start | bytes 4718592 | tf_op jit(solution)/shard_map/all_gather | solution.py:75
  177.9 52.9 %collective-permute-start.2 = (f32[128,1024]{1,0:T(8,128)S(1)}, f32[128,1024]{1,0:T(8,128)S(1)}, u32[]{:S(2)}, u32[]{:S(2)}) collective-permute-start(f32[128,1024]{1,0:T(8,128)S(1)} %fusion.20), channel_id=1, source_target_pairs={{0,32},{8,40},{16,48},{24,56},{32,0},{40,8},{48,16},{56,24},{64,96... | collective-permute-start | bytes 1572872 | tf_op jit(solution)/shard_map/ppermute | solution.py:11
  231.7 192.3 %copy-start.2 = (f32[32,128]{1,0:T(8,128)S(1)}, f32[32,128]{1,0:T(8,128)}, u32[]{:S(2)}) copy-start(f32[32,128]{1,0:T(8,128)} %param.8) | copy-start | bytes 49156
  231.7 83.0 %reduce-scatter.9.cloned.1.call-start = ((), (), s32[]{:S(2)}) async-start(), calls=%async_computation.12 | async-start | bytes 147456 | tf_op jit(solution)/shard_map/reduce_scatter | solution.py:103
  277.9 90.7 %reduce-scatter.11.cloned.1.call-start = ((), (), s32[]{:S(2)}) async-start(), calls=%async_computation.13 | async-start | bytes 147456 | tf_op jit(solution)/shard_map/reduce_scatter | solution.py:103
  314.7 13.4 %collective-permute-start.10 = (f32[32,128]{1,0:T(8,128)}, f32[32,128]{1,0:T(8,128)S(1)}, u32[]{:S(2)}, u32[]{:S(2)}) collective-permute-start(f32[32,128]{1,0:T(8,128)} %reduce-scatter.9.cloned.1.call-done), channel_id=1, source_target_pairs={{64,0},{72,8},{80,16},{88,24},{96,32},{104,40},{112,48},{120,56},{... | collective-permute-start | bytes 49160 | tf_op jit(solution)/shard_map/ppermute | solution.py:17
  329.1 93.5 %reduce-scatter.13.cloned.1.call-start = ((), (), s32[]{:S(2)}) async-start(), calls=%async_computation.14 | async-start | bytes 147456 | tf_op jit(solution)/shard_map/reduce_scatter | solution.py:103
  368.7 13.4 %collective-permute-start.11 = (f32[32,128]{1,0:T(8,128)}, f32[32,128]{1,0:T(8,128)S(1)}, u32[]{:S(2)}, u32[]{:S(2)}) collective-permute-start(f32[32,128]{1,0:T(8,128)} %reduce-scatter.11.cloned.1.call-done), channel_id=1, source_target_pairs={{64,0},{72,8},{80,16},{88,24},{96,32},{104,40},{112,48},{120,56},{... | collective-permute-start | bytes 49160 | tf_op jit(solution)/shard_map/ppermute | solution.py:17
  383.1 95.1 %reduce-scatter.15.cloned.1.call-start = ((), (), s32[]{:S(2)}) async-start(), calls=%async_computation.15 | async-start | bytes 147456 | tf_op jit(solution)/shard_map/reduce_scatter | solution.py:103
  422.7 16.2 %collective-permute-start.12 = (f32[32,128]{1,0:T(8,128)}, f32[32,128]{1,0:T(8,128)S(1)}, u32[]{:S(2)}, u32[]{:S(2)}) collective-permute-start(f32[32,128]{1,0:T(8,128)} %reduce-scatter.13.cloned.1.call-done), channel_id=1, source_target_pairs={{64,0},{72,8},{80,16},{88,24},{96,32},{104,40},{112,48},{120,56},{... | collective-permute-start | bytes 49160 | tf_op jit(solution)/shard_map/ppermute | solution.py:17
  440.0 93.2 %reduce-scatter.17.cloned.1.call-start = ((), (), s32[]{:S(2)}) async-start(), calls=%async_computation.16 | async-start | bytes 147456 | tf_op jit(solution)/shard_map/reduce_scatter | solution.py:103
  440.6 14.0 %collective-permute-start.3 = (f32[32,128]{1,0:T(8,128)S(1)}, f32[32,128]{1,0:T(8,128)S(1)}, u32[]{:S(2)}, u32[]{:S(2)}) collective-permute-start(f32[32,128]{1,0:T(8,128)S(1)} %convolution_bitcast_fusion.1), channel_id=1, source_target_pairs={{0,64},{8,72},{16,80},{24,88},{32,96},{40,104},{48,112},{56,120},{... | collective-permute-start | bytes 49160 | tf_op jit(solution)/shard_map/ppermute | solution.py:17
  478.2 14.8 %collective-permute-start.13 = (f32[32,128]{1,0:T(8,128)}, f32[32,128]{1,0:T(8,128)S(1)}, u32[]{:S(2)}, u32[]{:S(2)}) collective-permute-start(f32[32,128]{1,0:T(8,128)} %reduce-scatter.15.cloned.1.call-done), channel_id=1, source_target_pairs={{64,0},{72,8},{80,16},{88,24},{96,32},{104,40},{112,48},{120,56},{... | collective-permute-start | bytes 49160 | tf_op jit(solution)/shard_map/ppermute | solution.py:17
  480.1 218.9 %copy-start.3 = (f32[32,128]{1,0:T(8,128)S(1)}, f32[32,128]{1,0:T(8,128)}, u32[]{:S(2)}) copy-start(f32[32,128]{1,0:T(8,128)} %reduce-scatter.9.cloned.1.call-done) | copy-start | bytes 49156
  480.1 218.9 %copy-start.4 = (f32[32,128]{1,0:T(8,128)S(1)}, f32[32,128]{1,0:T(8,128)}, u32[]{:S(2)}) copy-start(f32[32,128]{1,0:T(8,128)} %reduce-scatter.11.cloned.1.call-done) | copy-start | bytes 49156
  480.2 218.9 %copy-start.5 = (f32[32,128]{1,0:T(8,128)S(1)}, f32[32,128]{1,0:T(8,128)}, u32[]{:S(2)}) copy-start(f32[32,128]{1,0:T(8,128)} %reduce-scatter.13.cloned.1.call-done) | copy-start | bytes 49156
  480.2 218.9 %copy-start.6 = (f32[32,128]{1,0:T(8,128)S(1)}, f32[32,128]{1,0:T(8,128)}, u32[]{:S(2)}) copy-start(f32[32,128]{1,0:T(8,128)} %reduce-scatter.15.cloned.1.call-done) | copy-start | bytes 49156
  480.2 14.0 %collective-permute-start.4 = (f32[32,128]{1,0:T(8,128)S(1)}, f32[32,128]{1,0:T(8,128)S(1)}, u32[]{:S(2)}, u32[]{:S(2)}) collective-permute-start(f32[32,128]{1,0:T(8,128)S(1)} %fusion.35), channel_id=1, source_target_pairs={{0,64},{8,72},{16,80},{24,88},{32,96},{40,104},{48,112},{56,120},{... | collective-permute-start | bytes 49160 | tf_op jit(solution)/shard_map/ppermute | solution.py:17
  494.1 94.6 %reduce-scatter.19.cloned.1.call-start = ((), (), s32[]{:S(2)}) async-start(), calls=%async_computation.17 | async-start | bytes 147456 | tf_op jit(solution)/shard_map/reduce_scatter | solution.py:103
  510.7 23.9 %collective-permute-start.5 = (f32[32,128]{1,0:T(8,128)S(1)}, f32[32,128]{1,0:T(8,128)S(1)}, u32[]{:S(2)}, u32[]{:S(2)}) collective-permute-start(f32[32,128]{1,0:T(8,128)S(1)} %fusion.36), channel_id=1, source_target_pairs={{0,64},{8,72},{16,80},{24,88},{32,96},{40,104},{48,112},{56,120},{... | collective-permute-start | bytes 49160 | tf_op jit(solution)/shard_map/ppermute | solution.py:17
  533.2 165.9 %copy-start.7 = (f32[32,128]{1,0:T(8,128)S(1)}, f32[32,128]{1,0:T(8,128)}, u32[]{:S(2)}) copy-start(f32[32,128]{1,0:T(8,128)} %reduce-scatter.17.cloned.1.call-done) | copy-start | bytes 49156
  533.2 16.1 %collective-permute-start.14 = (f32[32,128]{1,0:T(8,128)}, f32[32,128]{1,0:T(8,128)S(1)}, u32[]{:S(2)}, u32[]{:S(2)}) collective-permute-start(f32[32,128]{1,0:T(8,128)} %reduce-scatter.17.cloned.1.call-done), channel_id=1, source_target_pairs={{64,0},{72,8},{80,16},{88,24},{96,32},{104,40},{112,48},{120,56},{... | collective-permute-start | bytes 49160 | tf_op jit(solution)/shard_map/ppermute | solution.py:17
  550.4 93.1 %reduce-scatter.21.cloned.1.call-start = ((), (), s32[]{:S(2)}) async-start(), calls=%async_computation.18 | async-start | bytes 147456 | tf_op jit(solution)/shard_map/reduce_scatter | solution.py:103
  551.0 14.0 %collective-permute-start.6 = (f32[32,128]{1,0:T(8,128)S(1)}, f32[32,128]{1,0:T(8,128)S(1)}, u32[]{:S(2)}, u32[]{:S(2)}) collective-permute-start(f32[32,128]{1,0:T(8,128)S(1)} %fusion.37), channel_id=1, source_target_pairs={{0,64},{8,72},{16,80},{24,88},{32,96},{40,104},{48,112},{56,120},{... | collective-permute-start | bytes 49160 | tf_op jit(solution)/shard_map/ppermute | solution.py:17
  588.7 110.3 %copy-start.8 = (f32[32,128]{1,0:T(8,128)S(1)}, f32[32,128]{1,0:T(8,128)}, u32[]{:S(2)}) copy-start(f32[32,128]{1,0:T(8,128)} %reduce-scatter.19.cloned.1.call-done) | copy-start | bytes 49156
  588.7 14.8 %collective-permute-start.15 = (f32[32,128]{1,0:T(8,128)}, f32[32,128]{1,0:T(8,128)S(1)}, u32[]{:S(2)}, u32[]{:S(2)}) collective-permute-start(f32[32,128]{1,0:T(8,128)} %reduce-scatter.19.cloned.1.call-done), channel_id=1, source_target_pairs={{64,0},{72,8},{80,16},{88,24},{96,32},{104,40},{112,48},{120,56},{... | collective-permute-start | bytes 49160 | tf_op jit(solution)/shard_map/ppermute | solution.py:17
  590.8 13.8 %collective-permute-start.7 = (f32[32,128]{1,0:T(8,128)S(1)}, f32[32,128]{1,0:T(8,128)S(1)}, u32[]{:S(2)}, u32[]{:S(2)}) collective-permute-start(f32[32,128]{1,0:T(8,128)S(1)} %fusion.38), channel_id=1, source_target_pairs={{0,64},{8,72},{16,80},{24,88},{32,96},{40,104},{48,112},{56,120},{... | collective-permute-start | bytes 49160 | tf_op jit(solution)/shard_map/ppermute | solution.py:17
  604.6 94.4 %reduce-scatter.23.cloned.1.call-start = ((), (), s32[]{:S(2)}) async-start(), calls=%async_computation.19 | async-start | bytes 147456 | tf_op jit(solution)/shard_map/reduce_scatter | solution.py:103
  621.2 23.6 %collective-permute-start.8 = (f32[32,128]{1,0:T(8,128)S(1)}, f32[32,128]{1,0:T(8,128)S(1)}, u32[]{:S(2)}, u32[]{:S(2)}) collective-permute-start(f32[32,128]{1,0:T(8,128)S(1)} %fusion.39), channel_id=1, source_target_pairs={{0,64},{8,72},{16,80},{24,88},{32,96},{40,104},{48,112},{56,120},{... | collective-permute-start | bytes 49160 | tf_op jit(solution)/shard_map/ppermute | solution.py:17
  643.5 16.0 %collective-permute-start.16 = (f32[32,128]{1,0:T(8,128)}, f32[32,128]{1,0:T(8,128)S(1)}, u32[]{:S(2)}, u32[]{:S(2)}) collective-permute-start(f32[32,128]{1,0:T(8,128)} %reduce-scatter.21.cloned.1.call-done), channel_id=1, source_target_pairs={{64,0},{72,8},{80,16},{88,24},{96,32},{104,40},{112,48},{120,56},{... | collective-permute-start | bytes 49160 | tf_op jit(solution)/shard_map/ppermute | solution.py:17
  661.2 14.1 %collective-permute-start.9 = (f32[32,128]{1,0:T(8,128)S(1)}, f32[32,128]{1,0:T(8,128)S(1)}, u32[]{:S(2)}, u32[]{:S(2)}) collective-permute-start(f32[32,128]{1,0:T(8,128)S(1)} %fusion.40), channel_id=1, source_target_pairs={{0,64},{8,72},{16,80},{24,88},{32,96},{40,104},{48,112},{56,120},{... | collective-permute-start | bytes 49160 | tf_op jit(solution)/shard_map/ppermute | solution.py:17
Sparse Core Ops, SparseCore 0:
  10.6 38.6 all-gather.4
  67.6 34.2 all-gather.6
  132.2 41.0 all-gather.8
  231.8 40.4 all-gather.10
  278.1 36.5 reduce-scatter.8
  329.3 39.3 reduce-scatter.10
  383.3 39.3 reduce-scatter.12
  440.1 38.0 reduce-scatter.14
  494.2 38.8 reduce-scatter.16
  550.5 38.1 reduce-scatter.18
  604.7 38.7 reduce-scatter.20
  660.7 38.2 reduce-scatter.22
where the time goes:
time: 710 us; the launch traced here: 707 us
  waiting for transfers between devices  417 us (59%)
  blocking collectives  120 us (17%)
  starting transfers between devices  116 us (16%)
  matrix products  33 us (5%)
  between operations  16 us (2%)
    reduce_scatter x8, waiting for transfers between devices, on_device(): lax.psum_scatter(partial_term, 'row', scatter_dimension=1, tiled=True)  160 us
    all_gather x8, blocking collectives, on_device(): lax.all_gather(forward_field, 'row', axis=1, tiled=True)  120 us
    ppermute x14, starting transfers between devices, from_behind(): return lax.ppermute(block, axis, route)  101 us
    all_gather x2, waiting for transfers between devices, on_device(): lax.all_gather(earlier_level, 'row', axis=0, tiled=True)  81.7 us
    ppermute x3, waiting for transfers between devices, partner(): lax.ppermute(array, axis, [(i, i ^ 1 << bit) for i in range(lax.axis_size...  74.8 us
    all_gather x1, waiting for transfers between devices, on_device(): whole_band = lax.all_gather(banded, 'row', axis=0, tiled=True)  38.8 us
    all_gather x1, waiting for transfers between devices, on_device(): lax.all_gather(earlier_map, 'row', axis=0, tiled=True)  34.4 us
    ppermute x14, waiting for transfers between devices, from_behind(): return lax.ppermute(block, axis, route)  26.8 us
  transfers between devices with their start and end apart: 29, of which 20 were waited for; matrix products, arithmetic and copies ran while one was open for 1% of the time, Pallas kernels for 0%

commit v1 on v0

v1 whole, which is shorter than its diff:
```python
import jax
import jax.numpy as jnp
from jax import lax
from jax.experimental import pallas as pl
from jax.experimental.pallas import tpu as pltpu
from jax.sharding import PartitionSpec as P

MESH = pl.DeviceIdType.MESH
BLOCK = 16
GROUP = 8
GROUPS = 8
ROWS = 8
PANELS = 4
ORDERS = 1024
TILE = 128
TILES = ORDERS // TILE
PANEL = ORDERS // PANELS
CHUNK = TILE + 16
FIELDS = 32
LINE = 2 * GROUP
REACH = 6
STRIP = 256
f32 = jnp.float32
bf16 = jnp.bfloat16


def role_layer(group, kind):
    odd = group % 2
    return LINE * (group // 2) + jnp.where(kind == 0, GROUP - 1 + odd, (LINE - 1) * odd)


def kernel(off_ref, width_ref, coupling_ref, incident_ref, cotangent_ref, sent_ref, back_ref,
           local, packs, flipped, banded, carry, even, odd, weights, field_in, chain_in, chain_out, spread, landed,
           load_sem, pack_send, pack_recv, ring_send, ring_recv, field_send, field_recv,
           chain_send, chain_recv, spread_send, spread_recv):
    layer = lax.axis_index("layer")
    row = lax.axis_index("row")
    y = row // 2
    core = row % 2
    group = layer // GROUP
    inner = layer % GROUP
    lead = (role_layer(group, 0), role_layer(group, 1))
    is_role = [(core == 0) & (layer == lead[0]), (core == 0) & (layer == lead[1])]
    role = is_role[0] | is_role[1]
    kind = jnp.where(layer == lead[1], 1, 0)
    place = jnp.where(kind == 0, group, GROUPS - 1 - group)
    first = place == 0
    final = place == GROUPS - 1
    follow = role_layer(jnp.where(kind == 0, jnp.minimum(group + 1, GROUPS - 1), jnp.maximum(group - 1, 0)), kind)
    precede = role_layer(jnp.where(kind == 0, jnp.maximum(group - 1, 0), jnp.minimum(group + 1, GROUPS - 1)), kind)
    start_layers = (role_layer(0, 0), role_layer(GROUPS - 1, 1))
    at_start = (layer == start_layers[0]) | (layer == start_layers[1])

    load = pltpu.make_async_copy(coupling_ref.at[0], local, load_sem.at[0])
    load.start()
    own_field = field_in.at[row]
    field_loads = [
        pltpu.make_async_copy(source, own_field, load_sem.at[1]) for source in (incident_ref, cotangent_ref)
    ]
    for which in range(2):
        @pl.when(layer == start_layers[which])
        def _(which=which):
            field_loads[which].start()

    barrier = pltpu.get_barrier_semaphore()

    def greet(to_layer, to_row):
        pl.semaphore_signal(barrier, inc=1, device_id={"layer": to_layer, "row": to_row}, device_id_type=MESH)

    for which in range(2):
        @pl.when(jnp.logical_not(is_role[which]))
        def _(which=which):
            greet(lead[which], 2 * y)

    @pl.when(role)
    def _():
        for i in range(GROUP):
            for c in range(2):
                @pl.when((i != inner) | (c != core))
                def _(i=i, c=c):
                    greet(GROUP * group + i, 2 * y + c)
        for step in range(1, PANELS):
            greet(layer, 2 * ((y + step) % PANELS))

        @pl.when(jnp.logical_not(first))
        def _():
            for p in range(PANELS):
                greet(precede, 2 * p)

        @pl.when(first)
        def _():
            for step in range(1, PANELS):
                greet(layer, 2 * ((y + step) % PANELS) + 1)

    load.wait()
    offset = off_ref[0].astype(f32)
    half_width = width_ref[0].astype(f32)
    block_row = lax.broadcasted_iota(jnp.int32, (TILE, TILE), 0) // BLOCK
    block_col = lax.broadcasted_iota(jnp.int32, (TILE, TILE), 1) // BLOCK
    relative = (block_col - block_row).astype(f32)
    ahead = (GROUP * row).astype(f32)
    folded = jnp.zeros((TILE, TILE), f32)
    for s in range(TILES):
        d = relative + (8.0 * s - ahead)
        upper = (d >= 0) & (jnp.abs(d - offset) <= half_width)
        folded = folded + jnp.where(upper, local[:, TILE * s:TILE * s + TILE].astype(f32), 0.0)
    packs[inner, row, 0:TILE, :] = folded.astype(bf16)
    tail = lax.broadcasted_iota(jnp.int32, (16, TILE), 0)
    packs[inner, row, TILE:CHUNK, :] = jnp.where(tail < 8, offset, half_width).astype(bf16)
    for which in range(2):
        @pl.when(layer == start_layers[which])
        def _(which=which):
            field_loads[which].wait()

    expected = jnp.where(role, 2 * GROUP + PANELS - 1 + jnp.where(final, 0, PANELS), 2)
    expected = expected + jnp.where(at_start & (core == 1), PANELS - 1, 0)
    pl.semaphore_wait(barrier, expected)

    def pack_copy(which, i, r, to_layer):
        return pltpu.make_async_remote_copy(
            src_ref=packs.at[i, r], dst_ref=packs.at[i, r],
            send_sem=pack_send.at[which], recv_sem=pack_recv.at[i, r % 2],
            device_id={"layer": to_layer, "row": 2 * y}, device_id_type=MESH)

    for which in range(2):
        @pl.when(jnp.logical_not(is_role[which]))
        def _(which=which):
            pack_copy(which, inner, row, lead[which]).start()

    def field_copy(step):
        return pltpu.make_async_remote_copy(
            src_ref=field_in.at[row], dst_ref=field_in.at[row],
            send_sem=field_send.at[step], recv_sem=field_recv.at[row],
            device_id={"layer": layer, "row": 2 * ((y + step) % PANELS)}, device_id_type=MESH)

    @pl.when(at_start)
    def _():
        for step in range(PANELS):
            @pl.when((core == 1) | (step != 0))
            def _(step=step):
                field_copy(step).start()

    def spread_copy(i, c, which):
        return pltpu.make_async_remote_copy(
            src_ref=spread.at[c], dst_ref=landed.at[which],
            send_sem=spread_send.at[i, c], recv_sem=spread_recv.at[which],
            device_id={"layer": GROUP * group + i, "row": 2 * y + c}, device_id_type=MESH)

    @pl.when(role)
    def _():
        forward_order = (kind == 1) != first
        sign = jnp.where(forward_order, 1.0, -1.0).astype(f32)

        def nth(k):
            return jnp.where(forward_order, k, GROUP - 1 - k)

        def ring_copy(i, step):
            other = 2 * ((y + step) % PANELS)
            return pltpu.make_async_remote_copy(
                src_ref=packs.at[i, pl.ds(2 * y, 2)], dst_ref=packs.at[i, pl.ds(2 * y, 2)],
                send_sem=ring_send.at[i, step], recv_sem=ring_recv.at[i, y],
                device_id={"layer": layer, "row": other}, device_id_type=MESH)

        def ring_arrival(i, step):
            source = (y + step) % PANELS
            return pltpu.make_async_remote_copy(
                src_ref=packs.at[i, pl.ds(2 * source, 2)], dst_ref=packs.at[i, pl.ds(2 * source, 2)],
                send_sem=ring_send.at[i, step], recv_sem=ring_recv.at[i, source],
                device_id={"layer": layer, "row": 2 * source}, device_id_type=MESH)

        def pass_round(k):
            i = nth(k)

            @pl.when(i != inner)
            def _():
                pack_copy(0, i, 2 * y, lead[0]).wait_recv()
            pack_copy(0, i, 2 * y + 1, lead[0]).wait_recv()
            for step in range(1, PANELS):
                ring_copy(i, step).start()

        pass_round(0)
        pass_round(1)

        @pl.when(first)
        def _():
            for r in range(ROWS):
                @pl.when(r != row)
                def _(r=r):
                    pltpu.make_async_remote_copy(
                        src_ref=field_in.at[r], dst_ref=field_in.at[r],
                        send_sem=field_send.at[0], recv_sem=field_recv.at[r],
                        device_id={"layer": layer, "row": (row + 1) % ROWS}, device_id_type=MESH).wait_recv()
                tall = jnp.concatenate([field_in[r], jnp.zeros((TILE - FIELDS, TILE), f32)], axis=0)
                carry[TILE * r:TILE * r + TILE, 0:TILE] = tall.T
            carry[:, TILE:PANEL] = jnp.zeros((ORDERS, PANEL - TILE), f32)

        @pl.when(jnp.logical_not(first))
        def _():
            rows_at = lax.broadcasted_iota(jnp.int32, (ORDERS, PANEL), 0)
            cols_at = lax.broadcasted_iota(jnp.int32, (ORDERS, PANEL), 1)
            carry[...] = jnp.where(rows_at == cols_at + PANEL * y, 1.0, 0.0).astype(f32)

        even[...] = carry[...].astype(bf16)
        blank = jnp.zeros((TILE, TILE), bf16)

        @pl.loop(0, GROUP)
        def _(k):
            @pl.when(k + 2 < GROUP)
            def _():
                pass_round(k + 2)
            i = nth(k)
            for step in range(1, PANELS):
                ring_arrival(i, step).wait_recv()
            off = packs[i, 0, TILE:TILE + 1, :].astype(f32)
            wide = packs[i, 0, TILE + 8:TILE + 9, :].astype(f32)

            def upper_mask(apart):
                d = relative + 8.0 * apart
                return jnp.where((d >= 0) & (jnp.abs(d - off) <= wide), 1.0, 0.0).astype(bf16)

            def lower_mask(apart):
                d = relative - 8.0 * apart
                return jnp.where((d < 0) & (jnp.abs(d + off) <= wide), -1.0, 0.0).astype(bf16)

            uppers = [upper_mask(apart) for apart in range(REACH)]
            lowers = [lower_mask(apart) for apart in range(REACH)]
            for t in range(TILES):
                flipped[:, TILE * t:TILE * t + TILE] = packs[i, t, 0:TILE, :].T
            for t in range(TILES):
                for s in range(TILES):
                    there = slice(TILE * s, TILE * s + TILE)
                    if abs(s - t) >= REACH:
                        value = blank
                    elif s > t:
                        value = packs[i, t, 0:TILE, :] * uppers[s - t]
                    elif s < t:
                        value = flipped[:, there] * lowers[t - s]
                    else:
                        value = packs[i, t, 0:TILE, :] * uppers[0] + flipped[:, there] * lowers[0]
                    banded[TILE * t:TILE * t + TILE, there] = value
            for divisor, source, target in ((4.0, even, odd), (3.0, odd, even), (2.0, even, odd), (1.0, odd, None)):
                for strip in range(0, ORDERS, STRIP):
                    here = slice(strip, strip + STRIP)
                    moved = jnp.dot(banded[here, :], source[...], preferred_element_type=f32)
                    total = carry[here, :] + moved * (sign / divisor)
                    if target is None:
                        carry[here, :] = total
                        even[here, :] = total.astype(bf16)
                    else:
                        target[here, :] = total.astype(bf16)

        @pl.when(first)
        def _():
            mine = carry[pl.ds(pl.multiple_of(PANEL * y, PANEL), PANEL), 0:TILE]
            chain_out[...] = mine.T[0:FIELDS, :]

        @pl.when(jnp.logical_not(first))
        def _():
            for strip in range(0, ORDERS, STRIP):
                here = slice(strip, strip + STRIP)
                value = carry[here, :]
                high = value.astype(bf16)
                weights[here, 0:PANEL] = high
                weights[here, PANEL:2 * PANEL] = (value - high.astype(f32)).astype(bf16)
            for p in range(PANELS):
                pltpu.make_async_remote_copy(
                    src_ref=chain_out, dst_ref=chain_in.at[p],
                    send_sem=chain_send.at[0], recv_sem=chain_recv.at[p],
                    device_id={"layer": precede, "row": 2 * p}, device_id_type=MESH).wait_recv()
            summed = jnp.zeros((2 * FIELDS, 2 * PANEL), f32)
            for p in range(PANELS):
                value = chain_in[p]
                high = value.astype(bf16)
                low = (value - high.astype(f32)).astype(bf16)
                both = jnp.concatenate([high, low], axis=0)
                summed = summed + jnp.dot(both, weights[PANEL * p:PANEL * p + PANEL, :], preferred_element_type=f32)
            chain_out[...] = (summed[0:FIELDS, 0:PANEL] + summed[FIELDS:, 0:PANEL]
                              + summed[0:FIELDS, PANEL:] + summed[FIELDS:, PANEL:])

        def chain_copy(p):
            return pltpu.make_async_remote_copy(
                src_ref=chain_out, dst_ref=chain_in.at[y],
                send_sem=chain_send.at[p], recv_sem=chain_recv.at[y],
                device_id={"layer": follow, "row": 2 * p}, device_id_type=MESH)

        @pl.when(jnp.logical_not(final))
        def _():
            for p in range(PANELS):
                chain_copy(p).start()

        for c in range(2):
            spread[c] = chain_out[:, TILE * c:TILE * c + TILE].astype(bf16)
        landed[kind] = spread[0]
        for i in range(GROUP):
            for c in range(2):
                @pl.when((i != inner) | (c != core))
                def _(i=i, c=c):
                    spread_copy(i, c, kind).start()

        for i in range(GROUP):
            for step in range(1, PANELS):
                ring_copy(i, step).wait_send()

        @pl.when(jnp.logical_not(final))
        def _():
            for p in range(PANELS):
                chain_copy(p).wait_send()
        for i in range(GROUP):
            for c in range(2):
                @pl.when((i != inner) | (c != core))
                def _(i=i, c=c):
                    spread_copy(i, c, kind).wait_send()

    for which in range(2):
        @pl.when(jnp.logical_not(is_role[which]))
        def _(which=which):
            pack_copy(which, inner, row, lead[which]).wait_send()

    @pl.when(at_start)
    def _():
        for step in range(PANELS):
            @pl.when((core == 1) | (step != 0))
            def _(step=step):
                field_copy(step).wait_send()

    for which, out in ((0, sent_ref), (1, back_ref)):
        @pl.when(jnp.logical_not(is_role[which]))
        def _(which=which):
            pltpu.make_async_remote_copy(
                src_ref=spread.at[0], dst_ref=landed.at[which],
                send_sem=spread_send.at[0, 0], recv_sem=spread_recv.at[which],
                device_id={"layer": lead[which], "row": 2 * y}, device_id_type=MESH).wait_recv()
        out[...] = landed[which]


def on_device(coupling, band_off, band_width, incident, cotangent):
    smem = pl.BlockSpec(memory_space=pltpu.SMEM)
    vmem = pl.BlockSpec(memory_space=pltpu.VMEM)
    away = pl.BlockSpec(memory_space=pl.ANY)
    dma = pltpu.SemaphoreType.DMA
    share = jax.ShapeDtypeStruct((FIELDS, TILE), bf16)
    sent, back = pl.pallas_call(
        kernel,
        out_shape=(share, share),
        in_specs=[smem, smem, away, away, away],
        out_specs=(vmem, vmem),
        scratch_shapes=[
            pltpu.VMEM((TILE, ORDERS), bf16),
            pltpu.VMEM((GROUP, ROWS, CHUNK, TILE), bf16),
            pltpu.VMEM((TILE, ORDERS), bf16),
            pltpu.VMEM((ORDERS, ORDERS), bf16),
            pltpu.VMEM((ORDERS, PANEL), f32),
            pltpu.VMEM((ORDERS, PANEL), bf16),
            pltpu.VMEM((ORDERS, PANEL), bf16),
            pltpu.VMEM((ORDERS, 2 * PANEL), bf16),
            pltpu.VMEM((ROWS, FIELDS, TILE), f32),
            pltpu.VMEM((PANELS, FIELDS, PANEL), f32),
            pltpu.VMEM((FIELDS, PANEL), f32),
            pltpu.VMEM((2, FIELDS, TILE), bf16),
            pltpu.VMEM((2, FIELDS, TILE), bf16),
            dma((2,)), dma((2,)), dma((GROUP, 2)), dma((GROUP, PANELS)), dma((GROUP, PANELS)),
            dma((PANELS,)), dma((ROWS,)), dma((PANELS,)), dma((PANELS,)), dma((GROUP, 2)), dma((2,)),
        ],
        compiler_params=pltpu.CompilerParams(collective_id=0, has_side_effects=True),
        name="cascade",
    )(band_off, band_width, coupling, incident, cotangent)
    return sent.astype(f32)[None], back.astype(f32)[None]


def solution(mesh):
    in_specs = (P("layer", "row", None), P("layer"), P("layer"), P(None, "row"), P(None, "row"))
    out_specs = (P("layer", None, "row"), P("layer", None, "row"))
    return jax.shard_map(
        on_device, mesh=mesh, in_specs=in_specs, out_specs=out_specs, check_vma=False
    )
```

time: 710 us -> 96.1 us (0.14)
  waiting for transfers between devices: 417 us -> 0 us
  blocking collectives: 120 us -> 0 us
  starting transfers between devices: 116 us -> 0 us
  Pallas kernels: 0 us -> 92.6 us
  matrix products: 33 us -> 0 us
  between operations: 16 us -> 1.93 us
    reduce_scatter x8 -> x0, waiting for transfers between devices: 160 us -> none  [on_device(): lax.psum_scatter(partial_term, 'row', scatter_dimension=1, tiled=True)]
    all_gather x4 -> x0, waiting for transfers between devices: 155 us -> none  [the longest x2 81.7 us: on_device(): lax.all_gather(earlier_level, 'row', axis=0, tiled=True)]
    all_gather x8 -> x0, blocking collectives: 120 us -> none  [on_device(): lax.all_gather(forward_field, 'row', axis=1, tiled=True)]
    ppermute x17 -> x0, starting transfers between devices: 116 us -> none  [the longest x14 101 us: from_behind(): return lax.ppermute(block, axis, route)]
    ppermute x17 -> x0, waiting for transfers between devices: 102 us -> none  [the longest x3 74.8 us: partner(): lax.ppermute(array, axis, [(i, i ^ 1 << bit) for i in range(lax.axis_size...]
    pallas_call x0 -> x1, Pallas kernels: none -> 92.6 us  [on_device(): pl.pallas_call(kernel, out_shape=(share, share), in_specs=[smem, smem, aw...]
    dot_general x21 -> x0, matrix products: 33 us -> none  [the longest x2 9.16 us: add_level(): jnp.dot(later_level, block_rows, precision=lax.Precision.HIGHEST, preferr...]
  transfers between devices with their start and end apart: 29 -> 0, of which waited for: 20 -> 0; matrix products, arithmetic and copies ran while one was open for 1% -> 0% of each run, Pallas kernels for 0% -> 0%
where the time goes in v1:
time: 96.1 us; the launch traced here: 95.9 us
  Pallas kernels  92.6 us (96%)
  between operations  1.93 us (2%)
  other arithmetic  1.33 us (1%)
    pallas_call x1, Pallas kernels, on_device(): pl.pallas_call(kernel, out_shape=(share, share), in_specs=[smem, smem, aw...  92.6 us

profile of v1, /device:TPU:1, one launch (start us, length us, event | category | flops | bytes accessed | tf_op | source)
XLA Modules:
  0.0 95.9 jit_solution(17653207900221614139)
XLA Ops:
  1.9 92.6 %cascade.1 = (bf16[32,128]{1,0:T(8,128)(2,1)}, bf16[32,128]{1,0:T(8,128)(2,1)}) custom-call(s32[1]{0:T(128)S(6)} %copy.7.off_ref, s32[1]{0:T(128)S(6)} %copy.8.width_ref, bf16[1,128,1024]{2,1,0:T(8,128)(2,1)} %coupling_ref.1, f32[32,128]{1,0:T(8,128)} %incident_ref.1, f32[32,128]{1,0:T(8,128)} %cotangent_ref.1), custom_call_target="tpu_custom_call" | custom-call | tf_op jit(solution)/shard_map/cascade/pallas_call | solution.py:342
  94.5 1.3 %bitcast_convert_fusion = (f32[1,32,128]{2,1,0:T(8,128)}, f32[1,32,128]{2,1,0:T(8,128)}) fusion(bf16[32,128]{1,0:T(8,128)(2,1)} %get-tuple-element.5, bf16[32,128]{1,0:T(8,128)(2,1)} %get-tuple-element.4), kind=kLoop, calls=%fused_computation | loop fusion | flops 8192 | bytes 49152 | tf_op jit(solution)/shard_map/broadcast_in_dim | solution.py:367

commit v2 on v1

v2 whole, which is shorter than its diff:
```python
import jax
import jax.numpy as jnp
from jax import lax
from jax.experimental import pallas as pl
from jax.experimental.pallas import tpu as pltpu
from jax.sharding import PartitionSpec as P

MESH = pl.DeviceIdType.MESH
BLOCK = 16
GROUP = 8
GROUPS = 8
ROWS = 8
PANELS = 4
ORDERS = 1024
TILE = 128
TILES = ORDERS // TILE
PANEL = ORDERS // PANELS
FIELDS = 32
LINE = 2 * GROUP
WIDEST = 3
WINDOW = 256
LEAD = 576
TRAIL = 640
PADDED = LEAD + ORDERS + TRAIL
SPAN = WINDOW // BLOCK
f32 = jnp.float32
bf16 = jnp.bfloat16


def role_layer(group, kind):
    return LINE * (group // 2) + jnp.where(kind == 0, GROUP - 1, 0)


def kernel(off_ref, width_ref, coupling_ref, incident_ref, cotangent_ref, sent_ref, back_ref,
           scalars, local, mine, note, packs, notes, offsets, plain, banded, carry, high, low, even, odd,
           field_in, chain_in, chain_out, landed,
           load_sem, pack_send, pack_recv, note_send, note_recv, note_load, ring_send, ring_recv,
           field_send, field_recv, chain_send, chain_recv, spread_send, spread_recv):
    layer = lax.axis_index("layer")
    row = lax.axis_index("row")
    y = row // 2
    core = row % 2
    place_z = layer % LINE
    pair = layer // LINE
    own_group = layer // GROUP
    inner = layer % GROUP
    parity = own_group % 2
    targets = ((role_layer(own_group, 0), 2 * y + parity), (role_layer(own_group, 1), 2 * y + parity))
    is_target = [(layer == targets[w][0]) & (row == targets[w][1]) for w in range(2)]
    inside = is_target[0] | is_target[1]
    role = (place_z == 0) | (place_z == GROUP - 1)
    kind = jnp.where(place_z == 0, 1, 0)
    group = 2 * pair + core
    place = jnp.where(kind == 0, group, GROUPS - 1 - group)
    first = place == 0
    final = place == GROUPS - 1
    ahead = jnp.where(kind == 0, jnp.minimum(group + 1, GROUPS - 1), jnp.maximum(group - 1, 0))
    behind = jnp.where(kind == 0, jnp.maximum(group - 1, 0), jnp.minimum(group + 1, GROUPS - 1))
    start_layers = (role_layer(0, 0), role_layer(GROUPS - 1, 1))
    at_start = (layer == start_layers[0]) | (layer == start_layers[1])
    start_core = jnp.where(layer == start_layers[0], 0, 1)
    up = (y + 1) % PANELS
    down = (y + PANELS - 1) % PANELS

    load = pltpu.make_async_copy(coupling_ref.at[0], local, load_sem.at[0])
    load.start()
    off_load = pltpu.make_async_copy(off_ref, scalars.at[0], load_sem.at[2])
    width_load = pltpu.make_async_copy(width_ref, scalars.at[1], load_sem.at[3])
    off_load.start()
    width_load.start()
    field_loads = [
        pltpu.make_async_copy(source, field_in.at[row], load_sem.at[1]) for source in (incident_ref, cotangent_ref)
    ]
    for which in range(2):
        @pl.when(layer == start_layers[which])
        def _(which=which):
            field_loads[which].start()

    barrier = pltpu.get_barrier_semaphore()

    def greet(to_layer, to_row):
        pl.semaphore_signal(barrier, inc=1, device_id={"layer": to_layer, "row": to_row}, device_id_type=MESH)

    for which in range(2):
        @pl.when(jnp.logical_not(is_target[which]))
        def _(which=which):
            greet(*targets[which])

    @pl.when(role)
    def _():
        for i in range(GROUP):
            for c in range(2):
                @pl.when((GROUP * group + i != layer) | (c != core))
                def _(i=i, c=c):
                    greet(GROUP * group + i, 2 * y + c)
        greet(layer, 2 * up + core)
        greet(layer, 2 * down + core)

        @pl.when(jnp.logical_not(first))
        def _():
            for p in range(PANELS):
                greet(role_layer(behind, kind), 2 * p + behind % 2)

        @pl.when(first)
        def _():
            for step in range(1, ROWS):
                greet(layer, (row + step) % ROWS)

        for buffer in (high, low, even, odd):
            buffer[0:LEAD // BLOCK] = jnp.zeros((LEAD // BLOCK, BLOCK, PANEL), bf16)
            buffer[(LEAD + ORDERS) // BLOCK:PADDED // BLOCK] = jnp.zeros((TRAIL // BLOCK, BLOCK, PANEL), bf16)
        plain[0:LEAD // BLOCK] = jnp.zeros((LEAD // BLOCK, BLOCK, TILE), bf16)
        plain[(LEAD + ORDERS) // BLOCK:PADDED // BLOCK] = jnp.zeros((TRAIL // BLOCK, BLOCK, TILE), bf16)

    off_load.wait()
    width_load.wait()
    offset = scalars[0, 0]
    half_width = scalars[1, 0]
    note[...] = jnp.full((8, TILE), offset, jnp.int32)
    load.wait()
    here_row = lax.broadcasted_iota(jnp.int32, (TILE, TILE), 0) + TILE * row
    here_col = lax.broadcasted_iota(jnp.int32, (TILE, TILE), 1)
    folded = jnp.zeros((TILE, TILE), f32)
    for s in range(TILES):
        there = here_col + TILE * s
        apart = there // BLOCK - here_row // BLOCK
        upper = (there > here_row) & (jnp.abs(apart - offset) <= half_width)
        folded = folded + jnp.where(upper, local[:, TILE * s:TILE * s + TILE].astype(f32), 0.0)
    mine[...] = folded.astype(bf16)

    @pl.when(inside)
    def _():
        packs[inner, row] = mine[...]

        @pl.when(core == 0)
        def _():
            notes[inner] = note[...]

    for which in range(2):
        @pl.when(layer == start_layers[which])
        def _(which=which):
            field_loads[which].wait()

    expected = jnp.where(inside, 1, 2)
    expected = expected + jnp.where(role, 2 * GROUP + 2 - jnp.where(inside, 1, 0) + jnp.where(final, 0, PANELS), 0)
    expected = expected + jnp.where(at_start, PANELS - jnp.where(core == start_core, 1, 0), 0)
    pl.semaphore_wait(barrier, expected)

    def pack_copy(which):
        return pltpu.make_async_remote_copy(
            src_ref=mine, dst_ref=packs.at[inner, row],
            send_sem=pack_send.at[which], recv_sem=pack_recv.at[inner, core],
            device_id={"layer": targets[which][0], "row": targets[which][1]}, device_id_type=MESH)

    def note_copy(which):
        return pltpu.make_async_remote_copy(
            src_ref=note, dst_ref=notes.at[inner],
            send_sem=note_send.at[which], recv_sem=note_recv.at[inner],
            device_id={"layer": targets[which][0], "row": targets[which][1]}, device_id_type=MESH)

    for which in range(2):
        @pl.when(jnp.logical_not(is_target[which]))
        def _(which=which):
            pack_copy(which).start()

            @pl.when(core == 0)
            def _():
                note_copy(which).start()

    def field_copy(step):
        return pltpu.make_async_remote_copy(
            src_ref=field_in.at[row], dst_ref=field_in.at[row],
            send_sem=field_send.at[step], recv_sem=field_recv.at[row],
            device_id={"layer": layer, "row": 2 * ((y + step) % PANELS) + start_core}, device_id_type=MESH)

    @pl.when(at_start)
    def _():
        for step in range(PANELS):
            @pl.when((core != start_core) | (step != 0))
            def _(step=step):
                field_copy(step).start()

    def spread_copy(i, c):
        return pltpu.make_async_remote_copy(
            src_ref=chain_out.at[:, pl.ds(TILE * c, TILE)], dst_ref=landed.at[kind],
            send_sem=spread_send.at[i, c], recv_sem=spread_recv.at[kind],
            device_id={"layer": GROUP * group + i, "row": 2 * y + c}, device_id_type=MESH)

    @pl.when(role)
    def _():
        forward_order = (kind == 1) != first
        sign = jnp.where(forward_order, 1.0, -1.0).astype(f32)

        def nth(k):
            return jnp.where(forward_order, k, GROUP - 1 - k)

        def local_pack(i, c):
            return (GROUP * group + i == layer) & (c == core)

        def wait_pack(i, c):
            @pl.when(jnp.logical_not(local_pack(i, c)))
            def _():
                pltpu.make_async_remote_copy(
                    src_ref=mine, dst_ref=packs.at[i, 2 * y + c],
                    send_sem=pack_send.at[0], recv_sem=pack_recv.at[i, c],
                    device_id={"layer": layer, "row": 2 * up + core}, device_id_type=MESH).wait_recv()

        def pair_copy(i, toward, slot):
            return pltpu.make_async_remote_copy(
                src_ref=packs.at[i, pl.ds(2 * y, 2)], dst_ref=packs.at[i, pl.ds(2 * y, 2)],
                send_sem=ring_send.at[i, slot], recv_sem=ring_recv.at[i, slot],
                device_id={"layer": layer, "row": 2 * toward + core}, device_id_type=MESH)

        def pair_wait(i, source, slot):
            pltpu.make_async_remote_copy(
                src_ref=packs.at[i, pl.ds(2 * source, 2)], dst_ref=packs.at[i, pl.ds(2 * source, 2)],
                send_sem=ring_send.at[i, slot], recv_sem=ring_recv.at[i, slot],
                device_id={"layer": layer, "row": 2 * source + core}, device_id_type=MESH).wait_recv()

        def half_copy(i, r, toward, slot):
            return pltpu.make_async_remote_copy(
                src_ref=packs.at[i, r], dst_ref=packs.at[i, r],
                send_sem=ring_send.at[i, slot], recv_sem=ring_recv.at[i, slot],
                device_id={"layer": layer, "row": 2 * toward + core}, device_id_type=MESH)

        across = (y + 2) % PANELS

        def send_round(k):
            i = nth(k)
            wait_pack(i, 0)
            wait_pack(i, 1)
            pair_copy(i, up, 0).start()
            pair_copy(i, down, 1).start()

        def relay_round(k):
            i = nth(k)
            pair_wait(i, down, 0)
            half_copy(i, 2 * down, up, 2).start()
            pair_wait(i, up, 1)
            half_copy(i, 2 * up + 1, down, 3).start()

        def finish_round(k):
            i = nth(k)
            half_copy(i, 2 * across, up, 2).wait_recv()
            half_copy(i, 2 * across + 1, down, 3).wait_recv()

        def note_fetch(i):
            return pltpu.make_async_copy(notes.at[i], offsets.at[i], note_load.at[i])

        send_round(0)
        send_round(1)

        @pl.when(first)
        def _():
            for r in range(ROWS):
                @pl.when(r != row)
                def _(r=r):
                    pltpu.make_async_remote_copy(
                        src_ref=field_in.at[r], dst_ref=field_in.at[r],
                        send_sem=field_send.at[0], recv_sem=field_recv.at[r],
                        device_id={"layer": layer, "row": (row + 1) % ROWS}, device_id_type=MESH).wait_recv()
                tall = jnp.concatenate([field_in[r], jnp.zeros((TILE - FIELDS, TILE), f32)], axis=0)
                carry[TILE * r:TILE * r + TILE, 0:TILE] = tall.T
            carry[:, TILE:PANEL] = jnp.zeros((ORDERS, PANEL - TILE), f32)

        @pl.when(jnp.logical_not(first))
        def _():
            rows_at = lax.broadcasted_iota(jnp.int32, (ORDERS, PANEL), 0)
            cols_at = lax.broadcasted_iota(jnp.int32, (ORDERS, PANEL), 1)
            carry[...] = jnp.where(rows_at == cols_at + PANEL * y, 1.0, 0.0).astype(f32)

        def blocks_of(t):
            return slice((LEAD + TILE * t) // BLOCK, (LEAD + TILE * t + TILE) // BLOCK)

        def split(t, value):
            here = blocks_of(t)
            top = value.astype(bf16)
            high[here] = top.reshape(TILE // BLOCK, BLOCK, PANEL)
            low[here] = (value - top.astype(f32)).astype(bf16).reshape(TILE // BLOCK, BLOCK, PANEL)

        for t in range(TILES):
            split(t, carry[TILE * t:TILE * t + TILE, :])

        slot = lax.broadcasted_iota(jnp.int32, (TILE, WINDOW), 1) // BLOCK
        step = lax.broadcasted_iota(jnp.int32, (TILE, WINDOW), 0) // BLOCK
        near = jnp.abs(slot - step - WIDEST) <= WIDEST
        upper_mask = jnp.where(near, sign, 0.0).astype(bf16)
        lower_mask = jnp.where(near, -sign, 0.0).astype(bf16)

        relay_round(0)

        @pl.loop(0, GROUP)
        def _(k):
            @pl.when(k + 2 < GROUP)
            def _():
                send_round(k + 2)

            @pl.when(k + 1 < GROUP)
            def _():
                relay_round(k + 1)
            i = nth(k)

            @pl.when(jnp.logical_not(local_pack(i, 0)))
            def _():
                pltpu.make_async_remote_copy(
                    src_ref=note, dst_ref=notes.at[i],
                    send_sem=note_send.at[0], recv_sem=note_recv.at[i],
                    device_id={"layer": layer, "row": 2 * up + core}, device_id_type=MESH).wait_recv()
            note_fetch(i).start()
            finish_round(k)
            note_fetch(i).wait()
            off = offsets[i, 0, 0]
            turn = jnp.broadcast_to(WIDEST + 40 - notes[i, 0:1, :], (TILE, TILE))
            turns = [(turn & (1 << bit)) != 0 for bit in range(3)]

            def upper_at(t):
                return pl.ds((LEAD + TILE * t) // BLOCK - WIDEST + off, SPAN)

            def lower_at(t):
                return pl.ds((LEAD + TILE * t) // BLOCK - WIDEST - off, SPAN)

            for t in range(TILES):
                value = packs[i, t]
                plain[blocks_of(t)] = value.reshape(TILE // BLOCK, BLOCK, TILE)
                turned = value.astype(f32)
                for bit in range(3):
                    turned = jnp.where(turns[bit], pltpu.roll(turned, BLOCK << bit, 1), turned)
                turned = turned.astype(bf16)
                banded[t, :, 0:WINDOW] = jnp.concatenate([turned, turned], axis=1) * upper_mask
            for t in range(TILES):
                banded[t, :, WINDOW:2 * WINDOW] = plain[lower_at(t)].reshape(WINDOW, TILE).T * lower_mask

            def product(t, source):
                return (jnp.dot(banded[t, :, 0:WINDOW], source[upper_at(t)].reshape(WINDOW, PANEL), preferred_element_type=f32)
                        + jnp.dot(banded[t, :, WINDOW:2 * WINDOW], source[lower_at(t)].reshape(WINDOW, PANEL), preferred_element_type=f32))

            for order, source, target in ((1, high, even), (2, even, odd), (3, odd, even), (4, even, None)):
                for t in range(TILES):
                    here = slice(TILE * t, TILE * t + TILE)
                    term = product(t, source)
                    if order == 1:
                        term = term + product(t, low)
                    else:
                        term = term * (1.0 / order)
                    total = carry[here, :] + term
                    carry[here, :] = total
                    if target is None:
                        split(t, total)
                    else:
                        target[blocks_of(t)] = term.astype(bf16).reshape(TILE // BLOCK, BLOCK, PANEL)

        @pl.when(first)
        def _():
            part = carry[pl.ds(pl.multiple_of(PANEL * y, PANEL), PANEL), 0:TILE]
            chain_out[...] = part.T[0:FIELDS, :].astype(bf16)

        @pl.when(jnp.logical_not(first))
        def _():
            summed = jnp.zeros((FIELDS, PANEL), f32)
            for p in range(PANELS):
                pltpu.make_async_remote_copy(
                    src_ref=chain_out, dst_ref=chain_in.at[p],
                    send_sem=chain_send.at[0], recv_sem=chain_recv.at[p],
                    device_id={"layer": layer, "row": 2 * up + core}, device_id_type=MESH).wait_recv()
                summed = summed + jnp.dot(chain_in[p], high[(LEAD + PANEL * p) // BLOCK:(LEAD + PANEL * p + PANEL) // BLOCK].reshape(PANEL, PANEL),
                                          preferred_element_type=f32)
            chain_out[...] = summed.astype(bf16)

        def chain_copy(p):
            return pltpu.make_async_remote_copy(
                src_ref=chain_out, dst_ref=chain_in.at[y],
                send_sem=chain_send.at[p], recv_sem=chain_recv.at[y],
                device_id={"layer": role_layer(ahead, kind), "row": 2 * p + ahead % 2}, device_id_type=MESH)

        @pl.when(jnp.logical_not(final))
        def _():
            for p in range(PANELS):
                chain_copy(p).start()

        for i in range(GROUP):
            for c in range(2):
                @pl.when(jnp.logical_not(local_pack(i, c)))
                def _(i=i, c=c):
                    spread_copy(i, c).start()

        @pl.when(inside)
        def _():
            landed[kind] = jnp.where(core == 0, chain_out[:, 0:TILE], chain_out[:, TILE:PANEL])

        for i in range(GROUP):
            pair_copy(i, up, 0).wait_send()
            pair_copy(i, down, 1).wait_send()
            half_copy(i, 2 * down, up, 2).wait_send()
            half_copy(i, 2 * up + 1, down, 3).wait_send()

        @pl.when(jnp.logical_not(final))
        def _():
            for p in range(PANELS):
                chain_copy(p).wait_send()
        for i in range(GROUP):
            for c in range(2):
                @pl.when(jnp.logical_not(local_pack(i, c)))
                def _(i=i, c=c):
                    spread_copy(i, c).wait_send()

    for which in range(2):
        @pl.when(jnp.logical_not(is_target[which]))
        def _(which=which):
            pack_copy(which).wait_send()

            @pl.when(core == 0)
            def _():
                note_copy(which).wait_send()

    @pl.when(at_start)
    def _():
        for step in range(PANELS):
            @pl.when((core != start_core) | (step != 0))
            def _(step=step):
                field_copy(step).wait_send()

    for which, out in ((0, sent_ref), (1, back_ref)):
        @pl.when(jnp.logical_not(is_target[which]))
        def _(which=which):
            pltpu.make_async_remote_copy(
                src_ref=chain_out.at[:, pl.ds(0, TILE)], dst_ref=landed.at[which],
                send_sem=spread_send.at[0, 0], recv_sem=spread_recv.at[which],
                device_id={"layer": targets[which][0], "row": targets[which][1]}, device_id_type=MESH).wait_recv()
        out[...] = landed[which]


def on_device(coupling, band_off, band_width, incident, cotangent):
    vmem = pl.BlockSpec(memory_space=pltpu.VMEM)
    away = pl.BlockSpec(memory_space=pl.ANY)
    dma = pltpu.SemaphoreType.DMA
    share = jax.ShapeDtypeStruct((FIELDS, TILE), bf16)
    sent, back = pl.pallas_call(
        kernel,
        out_shape=(share, share),
        in_specs=[away] * 5,
        out_specs=(vmem, vmem),
        scratch_shapes=[
            pltpu.SMEM((2, 1), jnp.int32),
            pltpu.VMEM((TILE, ORDERS), bf16),
            pltpu.VMEM((TILE, TILE), bf16),
            pltpu.VMEM((8, TILE), jnp.int32),
            pltpu.VMEM((GROUP, ROWS, TILE, TILE), bf16),
            pltpu.VMEM((GROUP, 8, TILE), jnp.int32),
            pltpu.SMEM((GROUP, 8, TILE), jnp.int32),
            pltpu.VMEM((PADDED // BLOCK, BLOCK, TILE), bf16),
            pltpu.VMEM((TILES, TILE, 2 * WINDOW), bf16),
            pltpu.VMEM((ORDERS, PANEL), f32),
            pltpu.VMEM((PADDED // BLOCK, BLOCK, PANEL), bf16),
            pltpu.VMEM((PADDED // BLOCK, BLOCK, PANEL), bf16),
            pltpu.VMEM((PADDED // BLOCK, BLOCK, PANEL), bf16),
            pltpu.VMEM((PADDED // BLOCK, BLOCK, PANEL), bf16),
            pltpu.VMEM((ROWS, FIELDS, TILE), f32),
            pltpu.VMEM((PANELS, FIELDS, PANEL), bf16),
            pltpu.VMEM((FIELDS, PANEL), bf16),
            pltpu.VMEM((2, FIELDS, TILE), bf16),
            dma((4,)), dma((2,)), dma((GROUP, 2)), dma((2,)), dma((GROUP,)), dma((GROUP,)),
            dma((GROUP, 4)), dma((GROUP, 4)), dma((PANELS,)), dma((ROWS,)), dma((PANELS,)), dma((PANELS,)),
            dma((GROUP, 2)), dma((2,)),
        ],
        compiler_params=pltpu.CompilerParams(collective_id=0, has_side_effects=True),
        name="cascade",
    )(band_off, band_width, coupling, incident, cotangent)
    return sent.astype(f32)[None], back.astype(f32)[None]


def solution(mesh):
    in_specs = (P("layer", "row", None), P("layer"), P("layer"), P(None, "row"), P(None, "row"))
    out_specs = (P("layer", None, "row"), P("layer", None, "row"))
    return jax.shard_map(
        on_device, mesh=mesh, in_specs=in_specs, out_specs=out_specs, check_vma=False
    )
```

time: 96.1 us -> 91.1 us (0.948); the launches traced: 95.9 us -> 89.6 us
  Pallas kernels: 92.6 us -> 86.3 us
    pallas_call x1, Pallas kernels: 92.6 us -> 86.3 us  [on_device(): pl.pallas_call(kernel, out_shape=(share, share), in_specs=[away] * 5, out...]
where the time goes in v2:
time: 91.1 us; the launch traced here: 89.6 us
  Pallas kernels  86.3 us (95%)
  between operations  1.93 us (2%)
  other arithmetic  1.33 us (1%)
    pallas_call x1, Pallas kernels, on_device(): pl.pallas_call(kernel, out_shape=(share, share), in_specs=[away] * 5, out...  86.3 us

profile of v2, /device:TPU:1, one launch (start us, length us, event | category | flops | bytes accessed | tf_op | source)
XLA Modules:
  0.0 89.6 jit_solution(5288444439850729317)
XLA Ops:
  1.9 86.3 %cascade.1 = (bf16[32,128]{1,0:T(8,128)(2,1)}, bf16[32,128]{1,0:T(8,128)(2,1)}) custom-call(s32[1]{0:T(128)S(6)} %copy.7.off_ref, s32[1]{0:T(128)S(6)} %copy.8.width_ref, bf16[1,128,1024]{2,1,0:T(8,128)(2,1)} %coupling_ref.1, f32[32,128]{1,0:T(8,128)} %incident_ref.1, f32[32,128]{1,0:T(8,128)} %cotangent_ref.1), custom_call_target="tpu_custom_call" | custom-call | tf_op jit(solution)/shard_map/cascade/pallas_call | solution.py:437
  88.2 1.3 %bitcast_convert_fusion = (f32[1,32,128]{2,1,0:T(8,128)}, f32[1,32,128]{2,1,0:T(8,128)}) fusion(bf16[32,128]{1,0:T(8,128)(2,1)} %get-tuple-element.5, bf16[32,128]{1,0:T(8,128)(2,1)} %get-tuple-element.4), kind=kLoop, calls=%fused_computation | loop fusion | flops 8192 | bytes 49152 | tf_op jit(solution)/shard_map/broadcast_in_dim | solution.py:468

commit v3 on v2

--- a/solution.py
+++ b/solution.py
@@ -23,16 +23,25 @@
 TRAIL = 640
 PADDED = LEAD + ORDERS + TRAIL
 SPAN = WINDOW // BLOCK
+DIRECT = (0, 7)
+FORWARD_Z = 7
 f32 = jnp.float32
 bf16 = jnp.bfloat16
 
 
 def role_layer(group, kind):
-    return LINE * (group // 2) + jnp.where(kind == 0, GROUP - 1, 0)
+    return LINE * (group // 2) + jnp.where(kind == 0, FORWARD_Z, 0)
+
+
+def is_direct(i):
+    found = i == DIRECT[0]
+    for other in DIRECT[1:]:
+        found = found | (i == other)
+    return found
 
 
 def kernel(off_ref, width_ref, coupling_ref, incident_ref, cotangent_ref, sent_ref, back_ref,
-           scalars, local, mine, note, packs, notes, offsets, plain, banded, carry, high, low, even, odd,
+           scalars, local, mine, note, packs, notes, offsets, plain, flipped, banded, carry, high, low, even, odd,
            field_in, chain_in, chain_out, landed,
            load_sem, pack_send, pack_recv, note_send, note_recv, note_load, ring_send, ring_recv,
            field_send, field_recv, chain_send, chain_recv, spread_send, spread_recv):
@@ -48,7 +57,7 @@
     targets = ((role_layer(own_group, 0), 2 * y + parity), (role_layer(own_group, 1), 2 * y + parity))
     is_target = [(layer == targets[w][0]) & (row == targets[w][1]) for w in range(2)]
     inside = is_target[0] | is_target[1]
-    role = (place_z == 0) | (place_z == GROUP - 1)
+    role = (place_z == 0) | (place_z == FORWARD_Z)
     kind = jnp.where(place_z == 0, 1, 0)
     group = 2 * pair + core
     place = jnp.where(kind == 0, group, GROUPS - 1 - group)
@@ -89,10 +98,10 @@
     @pl.when(role)
     def _():
         for i in range(GROUP):
-            for c in range(2):
-                @pl.when((GROUP * group + i != layer) | (c != core))
-                def _(i=i, c=c):
-                    greet(GROUP * group + i, 2 * y + c)
+            for r in range(ROWS) if i in DIRECT else (2 * y, 2 * y + 1):
+                @pl.when((GROUP * group + i != layer) | (r != row))
+                def _(i=i, r=r):
+                    greet(GROUP * group + i, r)
         greet(layer, 2 * up + core)
         greet(layer, 2 * down + core)
 
@@ -126,6 +135,9 @@
         apart = there // BLOCK - here_row // BLOCK
         upper = (there > here_row) & (jnp.abs(apart - offset) <= half_width)
         folded = folded + jnp.where(upper, local[:, TILE * s:TILE * s + TILE].astype(f32), 0.0)
+    turn = jnp.broadcast_to(WIDEST + 40 - note[0:1, :], (TILE, TILE))
+    for bit in range(3):
+        folded = jnp.where((turn & (1 << bit)) != 0, pltpu.roll(folded, BLOCK << bit, 1), folded)
     mine[...] = folded.astype(bf16)
 
     @pl.when(inside)
@@ -141,16 +153,17 @@
         def _(which=which):
             field_loads[which].wait()
 
-    expected = jnp.where(inside, 1, 2)
+    direct = is_direct(inner)
+    expected = jnp.where(direct, 2 * PANELS, 2) - jnp.where(inside, 1, 0)
     expected = expected + jnp.where(role, 2 * GROUP + 2 - jnp.where(inside, 1, 0) + jnp.where(final, 0, PANELS), 0)
     expected = expected + jnp.where(at_start, PANELS - jnp.where(core == start_core, 1, 0), 0)
     pl.semaphore_wait(barrier, expected)
 
-    def pack_copy(which):
+    def pack_copy(which, step):
         return pltpu.make_async_remote_copy(
             src_ref=mine, dst_ref=packs.at[inner, row],
-            send_sem=pack_send.at[which], recv_sem=pack_recv.at[inner, core],
-            device_id={"layer": targets[which][0], "row": targets[which][1]}, device_id_type=MESH)
+            send_sem=pack_send.at[which, step], recv_sem=pack_recv.at[inner, row],
+            device_id={"layer": targets[which][0], "row": 2 * ((y + step) % PANELS) + parity}, device_id_type=MESH)
 
     def note_copy(which):
         return pltpu.make_async_remote_copy(
@@ -161,11 +174,17 @@
     for which in range(2):
         @pl.when(jnp.logical_not(is_target[which]))
         def _(which=which):
-            pack_copy(which).start()
+            pack_copy(which, 0).start()
 
             @pl.when(core == 0)
             def _():
                 note_copy(which).start()
+
+    @pl.when(direct)
+    def _():
+        for which in range(2):
+            for step in range(1, PANELS):
+                pack_copy(which, step).start()
 
     def field_copy(step):
         return pltpu.make_async_remote_copy(
@@ -197,12 +216,12 @@
         def local_pack(i, c):
             return (GROUP * group + i == layer) & (c == core)
 
-        def wait_pack(i, c):
-            @pl.when(jnp.logical_not(local_pack(i, c)))
+        def wait_pack(i, r):
+            @pl.when((GROUP * group + i != layer) | (r != row))
             def _():
                 pltpu.make_async_remote_copy(
-                    src_ref=mine, dst_ref=packs.at[i, 2 * y + c],
-                    send_sem=pack_send.at[0], recv_sem=pack_recv.at[i, c],
+                    src_ref=mine, dst_ref=packs.at[i, r],
+                    send_sem=pack_send.at[0, 0], recv_sem=pack_recv.at[i, r],
                     device_id={"layer": layer, "row": 2 * up + core}, device_id_type=MESH).wait_recv()
 
         def pair_copy(i, toward, slot):
@@ -227,25 +246,50 @@
 
         def send_round(k):
             i = nth(k)
-            wait_pack(i, 0)
-            wait_pack(i, 1)
-            pair_copy(i, up, 0).start()
-            pair_copy(i, down, 1).start()
+
+            @pl.when(jnp.logical_not(is_direct(i)))
+            def _():
+                wait_pack(i, 2 * y)
+                wait_pack(i, 2 * y + 1)
+                pair_copy(i, up, 0).start()
+                pair_copy(i, down, 1).start()
 
         def relay_round(k):
             i = nth(k)
-            pair_wait(i, down, 0)
-            half_copy(i, 2 * down, up, 2).start()
-            pair_wait(i, up, 1)
-            half_copy(i, 2 * up + 1, down, 3).start()
+
+            @pl.when(jnp.logical_not(is_direct(i)))
+            def _():
+                pair_wait(i, down, 0)
+                half_copy(i, 2 * down, up, 2).start()
+                pair_wait(i, up, 1)
+                half_copy(i, 2 * up + 1, down, 3).start()
 
         def finish_round(k):
             i = nth(k)
-            half_copy(i, 2 * across, up, 2).wait_recv()
-            half_copy(i, 2 * across + 1, down, 3).wait_recv()
+
+            @pl.when(jnp.logical_not(is_direct(i)))
+            def _():
+                half_copy(i, 2 * across, up, 2).wait_recv()
+                half_copy(i, 2 * across + 1, down, 3).wait_recv()
+
+            @pl.when(is_direct(i))
+            def _():
+                for r in range(ROWS):
+                    wait_pack(i, r)
 
         def note_fetch(i):
             return pltpu.make_async_copy(notes.at[i], offsets.at[i], note_load.at[i])
+
+        def note_round(k):
+            i = nth(k)
+
+            @pl.when(jnp.logical_not(local_pack(i, 0)))
+            def _():
+                pltpu.make_async_remote_copy(
+                    src_ref=note, dst_ref=notes.at[i],
+                    send_sem=note_send.at[0], recv_sem=note_recv.at[i],
+                    device_id={"layer": layer, "row": 2 * up + core}, device_id_type=MESH).wait_recv()
+            note_fetch(i).start()
 
         send_round(0)
         send_round(1)
@@ -287,6 +331,7 @@
         upper_mask = jnp.where(near, sign, 0.0).astype(bf16)
         lower_mask = jnp.where(near, -sign, 0.0).astype(bf16)
 
+        note_round(0)
         relay_round(0)
 
         @pl.loop(0, GROUP)
@@ -298,20 +343,15 @@
             @pl.when(k + 1 < GROUP)
             def _():
                 relay_round(k + 1)
+
+            @pl.when(k + 1 < GROUP)
+            def _():
+                note_round(k + 1)
             i = nth(k)
-
-            @pl.when(jnp.logical_not(local_pack(i, 0)))
-            def _():
-                pltpu.make_async_remote_copy(
-                    src_ref=note, dst_ref=notes.at[i],
-                    send_sem=note_send.at[0], recv_sem=note_recv.at[i],
-                    device_id={"layer": layer, "row": 2 * up + core}, device_id_type=MESH).wait_recv()
-            note_fetch(i).start()
             finish_round(k)
             note_fetch(i).wait()
             off = offsets[i, 0, 0]
-            turn = jnp.broadcast_to(WIDEST + 40 - notes[i, 0:1, :], (TILE, TILE))
-            turns = [(turn & (1 << bit)) != 0 for bit in range(3)]
+            turn = (WIDEST + 40 - off) % 8
 
             def upper_at(t):
                 return pl.ds((LEAD + TILE * t) // BLOCK - WIDEST + off, SPAN)
@@ -322,17 +362,19 @@
             for t in range(TILES):
                 value = packs[i, t]
                 plain[blocks_of(t)] = value.reshape(TILE // BLOCK, BLOCK, TILE)
-                turned = value.astype(f32)
-                for bit in range(3):
-                    turned = jnp.where(turns[bit], pltpu.roll(turned, BLOCK << bit, 1), turned)
-                turned = turned.astype(bf16)
-                banded[t, :, 0:WINDOW] = jnp.concatenate([turned, turned], axis=1) * upper_mask
+                banded[t, :, 0:WINDOW] = jnp.concatenate([value, value], axis=1) * upper_mask
             for t in range(TILES):
-                banded[t, :, WINDOW:2 * WINDOW] = plain[lower_at(t)].reshape(WINDOW, TILE).T * lower_mask
+                tall = plain[lower_at(t)].reshape(WINDOW, TILE).T.reshape(TILE // BLOCK, BLOCK, WINDOW)
+                flipped[t, 0:TILE // BLOCK] = tall
+                flipped[t, TILE // BLOCK:2 * TILE // BLOCK] = tall
+            for t in range(TILES):
+                tall = flipped[t, pl.ds(turn, TILE // BLOCK)].reshape(TILE, WINDOW)
+                banded[t, :, WINDOW:2 * WINDOW] = tall * lower_mask
 
             def product(t, source):
-                return (jnp.dot(banded[t, :, 0:WINDOW], source[upper_at(t)].reshape(WINDOW, PANEL), preferred_element_type=f32)
-                        + jnp.dot(banded[t, :, WINDOW:2 * WINDOW], source[lower_at(t)].reshape(WINDOW, PANEL), preferred_element_type=f32))
+                both = jnp.concatenate([source[upper_at(t)].reshape(WINDOW, PANEL),
+                                        source[lower_at(t)].reshape(WINDOW, PANEL)], axis=0)
+                return jnp.dot(banded[t], both, preferred_element_type=f32)
 
             for order, source, target in ((1, high, even), (2, even, odd), (3, odd, even), (4, even, None)):
                 for t in range(TILES):
@@ -387,7 +429,7 @@
         def _():
             landed[kind] = jnp.where(core == 0, chain_out[:, 0:TILE], chain_out[:, TILE:PANEL])
 
-        for i in range(GROUP):
+        for i in [j for j in range(GROUP) if j not in DIRECT]:
             pair_copy(i, up, 0).wait_send()
             pair_copy(i, down, 1).wait_send()
             half_copy(i, 2 * down, up, 2).wait_send()
@@ -406,11 +448,17 @@
     for which in range(2):
         @pl.when(jnp.logical_not(is_target[which]))
         def _(which=which):
-            pack_copy(which).wait_send()
+            pack_copy(which, 0).wait_send()
 
             @pl.when(core == 0)
             def _():
                 note_copy(which).wait_send()
+
+    @pl.when(direct)
+    def _():
+        for which in range(2):
+            for step in range(1, PANELS):
+                pack_copy(which, step).wait_send()
 
     @pl.when(at_start)
     def _():
@@ -448,6 +496,7 @@
             pltpu.VMEM((GROUP, 8, TILE), jnp.int32),
             pltpu.SMEM((GROUP, 8, TILE), jnp.int32),
             pltpu.VMEM((PADDED // BLOCK, BLOCK, TILE), bf16),
+            pltpu.VMEM((TILES, 2 * TILE // BLOCK, BLOCK, WINDOW), bf16),
             pltpu.VMEM((TILES, TILE, 2 * WINDOW), bf16),
             pltpu.VMEM((ORDERS, PANEL), f32),
             pltpu.VMEM((PADDED // BLOCK, BLOCK, PANEL), bf16),
@@ -458,7 +507,7 @@
             pltpu.VMEM((PANELS, FIELDS, PANEL), bf16),
             pltpu.VMEM((FIELDS, PANEL), bf16),
             pltpu.VMEM((2, FIELDS, TILE), bf16),
-            dma((4,)), dma((2,)), dma((GROUP, 2)), dma((2,)), dma((GROUP,)), dma((GROUP,)),
+            dma((4,)), dma((2, PANELS)), dma((GROUP, ROWS)), dma((2,)), dma((GROUP,)), dma((GROUP,)),
             dma((GROUP, 4)), dma((GROUP, 4)), dma((PANELS,)), dma((ROWS,)), dma((PANELS,)), dma((PANELS,)),
             dma((GROUP, 2)), dma((2,)),
         ],

time: 91.1 us -> 87.3 us (0.958); the launches traced: 89.6 us -> 87 us
  Pallas kernels: 86.3 us -> 83.8 us
    pallas_call x1, Pallas kernels: 86.3 us -> 83.8 us  [on_device(): pl.pallas_call(kernel, out_shape=(share, share), in_specs=[away] * 5, out...]
where the time goes in v3:
time: 87.3 us; the launch traced here: 87 us
  Pallas kernels  83.8 us (96%)
  between operations  1.93 us (2%)
  other arithmetic  1.33 us (2%)
    pallas_call x1, Pallas kernels, on_device(): pl.pallas_call(kernel, out_shape=(share, share), in_specs=[away] * 5, out...  83.8 us

profile of v3, /device:TPU:1, one launch (start us, length us, event | category | flops | bytes accessed | tf_op | source)
XLA Modules:
  0.0 87.0 jit_solution(4453163354564822843)
XLA Ops:
  1.9 83.8 %cascade.1 = (bf16[32,128]{1,0:T(8,128)(2,1)}, bf16[32,128]{1,0:T(8,128)(2,1)}) custom-call(s32[1]{0:T(128)S(6)} %copy.7.off_ref, s32[1]{0:T(128)S(6)} %copy.8.width_ref, bf16[1,128,1024]{2,1,0:T(8,128)(2,1)} %coupling_ref.1, f32[32,128]{1,0:T(8,128)} %incident_ref.1, f32[32,128]{1,0:T(8,128)} %cotangent_ref.1), custom_call_target="tpu_custom_call" | custom-call | tf_op jit(solution)/shard_map/cascade/pallas_call | solution.py:485
  85.7 1.3 %bitcast_convert_fusion = (f32[1,32,128]{2,1,0:T(8,128)}, f32[1,32,128]{2,1,0:T(8,128)}) fusion(bf16[32,128]{1,0:T(8,128)(2,1)} %get-tuple-element.5, bf16[32,128]{1,0:T(8,128)(2,1)} %get-tuple-element.4), kind=kLoop, calls=%fused_computation | loop fusion | flops 8192 | bytes 49152 | tf_op jit(solution)/shard_map/broadcast_in_dim | solution.py:517

commit v4 on v3

--- a/solution.py
+++ b/solution.py
@@ -23,7 +23,9 @@
 TRAIL = 640
 PADDED = LEAD + ORDERS + TRAIL
 SPAN = WINDOW // BLOCK
-DIRECT = (0, 7)
+SENDS_AHEAD = 4
+RELAYS_AHEAD = 2
+DIRECT = (GROUP,)
 FORWARD_Z = 7
 f32 = jnp.float32
 bf16 = jnp.bfloat16
@@ -154,6 +156,23 @@
             field_loads[which].wait()
 
     direct = is_direct(inner)
+    def blocks_of(t):
+        return slice((LEAD + TILE * t) // BLOCK, (LEAD + TILE * t + TILE) // BLOCK)
+
+    def split(t, value):
+        here = blocks_of(t)
+        top = value.astype(bf16)
+        high[here] = top.reshape(TILE // BLOCK, BLOCK, PANEL)
+        low[here] = (value - top.astype(f32)).astype(bf16).reshape(TILE // BLOCK, BLOCK, PANEL)
+
+    @pl.when(role & jnp.logical_not(first))
+    def _():
+        rows_at = lax.broadcasted_iota(jnp.int32, (ORDERS, PANEL), 0)
+        cols_at = lax.broadcasted_iota(jnp.int32, (ORDERS, PANEL), 1)
+        carry[...] = jnp.where(rows_at == cols_at + PANEL * y, 1.0, 0.0).astype(f32)
+        for t in range(TILES):
+            split(t, carry[TILE * t:TILE * t + TILE, :])
+
     expected = jnp.where(direct, 2 * PANELS, 2) - jnp.where(inside, 1, 0)
     expected = expected + jnp.where(role, 2 * GROUP + 2 - jnp.where(inside, 1, 0) + jnp.where(final, 0, PANELS), 0)
     expected = expected + jnp.where(at_start, PANELS - jnp.where(core == start_core, 1, 0), 0)
@@ -291,8 +310,11 @@
                     device_id={"layer": layer, "row": 2 * up + core}, device_id_type=MESH).wait_recv()
             note_fetch(i).start()
 
-        send_round(0)
-        send_round(1)
+        for k in range(SENDS_AHEAD):
+            send_round(k)
+        note_round(0)
+        for k in range(RELAYS_AHEAD):
+            relay_round(k)
 
         @pl.when(first)
         def _():
@@ -306,24 +328,8 @@
                 tall = jnp.concatenate([field_in[r], jnp.zeros((TILE - FIELDS, TILE), f32)], axis=0)
                 carry[TILE * r:TILE * r + TILE, 0:TILE] = tall.T
             carry[:, TILE:PANEL] = jnp.zeros((ORDERS, PANEL - TILE), f32)
-
-        @pl.when(jnp.logical_not(first))
-        def _():
-            rows_at = lax.broadcasted_iota(jnp.int32, (ORDERS, PANEL), 0)
-            cols_at = lax.broadcasted_iota(jnp.int32, (ORDERS, PANEL), 1)
-            carry[...] = jnp.where(rows_at == cols_at + PANEL * y, 1.0, 0.0).astype(f32)
-
-        def blocks_of(t):
-            return slice((LEAD + TILE * t) // BLOCK, (LEAD + TILE * t + TILE) // BLOCK)
-
-        def split(t, value):
-            here = blocks_of(t)
-            top = value.astype(bf16)
-            high[here] = top.reshape(TILE // BLOCK, BLOCK, PANEL)
-            low[here] = (value - top.astype(f32)).astype(bf16).reshape(TILE // BLOCK, BLOCK, PANEL)
-
-        for t in range(TILES):
-            split(t, carry[TILE * t:TILE * t + TILE, :])
+            for t in range(TILES):
+                split(t, carry[TILE * t:TILE * t + TILE, :])
 
         slot = lax.broadcasted_iota(jnp.int32, (TILE, WINDOW), 1) // BLOCK
         step = lax.broadcasted_iota(jnp.int32, (TILE, WINDOW), 0) // BLOCK
@@ -331,18 +337,15 @@
         upper_mask = jnp.where(near, sign, 0.0).astype(bf16)
         lower_mask = jnp.where(near, -sign, 0.0).astype(bf16)
 
-        note_round(0)
-        relay_round(0)
-
         @pl.loop(0, GROUP)
         def _(k):
-            @pl.when(k + 2 < GROUP)
-            def _():
-                send_round(k + 2)
-
-            @pl.when(k + 1 < GROUP)
-            def _():
-                relay_round(k + 1)
+            @pl.when(k + SENDS_AHEAD < GROUP)
+            def _():
+                send_round(k + SENDS_AHEAD)
+
+            @pl.when(k + RELAYS_AHEAD < GROUP)
+            def _():
+                relay_round(k + RELAYS_AHEAD)
 
             @pl.when(k + 1 < GROUP)
             def _():

time: 87.3 us -> 84.6 us (0.969)
  Pallas kernels: 83.8 us -> 81.1 us
    pallas_call x1, Pallas kernels: 83.8 us -> 81.1 us  [on_device(): pl.pallas_call(kernel, out_shape=(share, share), in_specs=[away] * 5, out...]
where the time goes in v4:
time: 84.6 us; the launch traced here: 84.4 us
  Pallas kernels  81.1 us (96%)
  between operations  1.93 us (2%)
  other arithmetic  1.33 us (2%)
    pallas_call x1, Pallas kernels, on_device(): pl.pallas_call(kernel, out_shape=(share, share), in_specs=[away] * 5, out...  81.1 us

profile of v4, /device:TPU:1, one launch (start us, length us, event | category | flops | bytes accessed | tf_op | source)
XLA Modules:
  0.0 84.4 jit_solution(430013655129249450)
XLA Ops:
  1.9 81.1 %cascade.1 = (bf16[32,128]{1,0:T(8,128)(2,1)}, bf16[32,128]{1,0:T(8,128)(2,1)}) custom-call(s32[1]{0:T(128)S(6)} %copy.7.off_ref, s32[1]{0:T(128)S(6)} %copy.8.width_ref, bf16[1,128,1024]{2,1,0:T(8,128)(2,1)} %coupling_ref.1, f32[32,128]{1,0:T(8,128)} %incident_ref.1, f32[32,128]{1,0:T(8,128)} %cotangent_ref.1), custom_call_target="tpu_custom_call" | custom-call | tf_op jit(solution)/shard_map/cascade/pallas_call | solution.py:488
  83.1 1.3 %bitcast_convert_fusion = (f32[1,32,128]{2,1,0:T(8,128)}, f32[1,32,128]{2,1,0:T(8,128)}) fusion(bf16[32,128]{1,0:T(8,128)(2,1)} %get-tuple-element.5, bf16[32,128]{1,0:T(8,128)(2,1)} %get-tuple-element.4), kind=kLoop, calls=%fused_computation | loop fusion | flops 8192 | bytes 49152 | tf_op jit(solution)/shard_map/broadcast_in_dim | solution.py:520

commit v5 on v4

--- a/solution.py
+++ b/solution.py
@@ -422,7 +422,7 @@
             for p in range(PANELS):
                 chain_copy(p).start()
 
-        for i in range(GROUP):
+        for i in reversed(range(GROUP)):
             for c in range(2):
                 @pl.when(jnp.logical_not(local_pack(i, c)))
                 def _(i=i, c=c):

time: 84.6 us -> 85.7 us (1.013); the launches traced: 84.4 us -> 84.6 us
  no operation moved by 1% of the time
where the time goes in v5:
time: 85.7 us; the launch traced here: 84.6 us
  Pallas kernels  81.4 us (95%)
  between operations  1.93 us (2%)
  other arithmetic  1.33 us (2%)
    pallas_call x1, Pallas kernels, on_device(): pl.pallas_call(kernel, out_shape=(share, share), in_specs=[away] * 5, out...  81.4 us

profile of v5, /device:TPU:1, one launch (start us, length us, event | category | flops | bytes accessed | tf_op | source)
XLA Modules:
  0.0 84.6 jit_solution(17459100624157037865)
XLA Ops:
  1.9 81.4 %cascade.1 = (bf16[32,128]{1,0:T(8,128)(2,1)}, bf16[32,128]{1,0:T(8,128)(2,1)}) custom-call(s32[1]{0:T(128)S(6)} %copy.7.off_ref, s32[1]{0:T(128)S(6)} %copy.8.width_ref, bf16[1,128,1024]{2,1,0:T(8,128)(2,1)} %coupling_ref.1, f32[32,128]{1,0:T(8,128)} %incident_ref.1, f32[32,128]{1,0:T(8,128)} %cotangent_ref.1), custom_call_target="tpu_custom_call" | custom-call | tf_op jit(solution)/shard_map/cascade/pallas_call | solution.py:488
  83.3 1.3 %bitcast_convert_fusion = (f32[1,32,128]{2,1,0:T(8,128)}, f32[1,32,128]{2,1,0:T(8,128)}) fusion(bf16[32,128]{1,0:T(8,128)(2,1)} %get-tuple-element.5, bf16[32,128]{1,0:T(8,128)(2,1)} %get-tuple-element.4), kind=kLoop, calls=%fused_computation | loop fusion | flops 8192 | bytes 49152 | tf_op jit(solution)/shard_map/broadcast_in_dim | solution.py:520
